TPU v7x, 256 devices: a whole 4x4x8 slice. The times are simulated.
256 devices in a mesh: fluid: 64 (over z, x_hi, y), grp: 4 (over x_lo, core).
Axes of the slice: x: 4 (x_hi: 2, x_lo: 2; x = x_hi * 2 + x_lo), y: 4, z: 8, core: 2. Of those that a mesh axis runs over, the one named last changes fastest.
Arguments:
- acoustic_modes: bfloat16 [2097152, 400], P(('fluid', 'grp')), may hold values from -6 to 6
- shell_modes: bfloat16 [65536, 300], P('fluid'), may hold values from -0.0004272461 to 0.0004272461
- wet_counts: int32 [256], P(('fluid', 'grp')), may hold values from 1 to 2048, 209715 in all
- fluid_nodes: int32 [524288], P(('fluid', 'grp')), may hold values from 0 to 8191
- shell_nodes: int32 [524288], P(('fluid', 'grp')), may hold values from 0 to 1023
- wet_area: float32 [524288], P(('fluid', 'grp')), may hold values from 0.15 to 0.6
- shell_freq: float32 [300], replicated, may hold values from 1 to 2
- shell_loss: float32 [300], replicated, may hold values from 0.2 to 0.5
- cavity_freq: float32 [400], replicated, may hold values from 1 to 2
- cavity_loss: float32 [400], replicated, may hold values from 0.2 to 0.5
- freqs: float32 [64], replicated, may hold values from 0.7 to 2.2
- modal_force: float32 [300], replicated, may hold values from -1.5 to 1.5
- cavity_source: float32 [400], replicated, may hold values from -1.5 to 1.5
Outputs:
- pressure: bfloat16 [2097152, 128], P(('fluid', 'grp'))
- modal_structure: float32 [2, 64, 300], P(None, 'grp')
Inputs may be any that keep to these rules, and one draw needn't show every extreme that they name: `wet_counts`: slots 0 to count - 1 of a device's 2048 interface slots are live, the others are ignored. `fluid_nodes`: numbered within the device's own 8192 cavity rows. `shell_nodes`: numbered within the 1024 shell rows of the device's fluid index.
All inputs are finite; a program needn't handle non-finite values.
Results may differ from a plain program's by a relative error of at most 0.0055.
Values may be sent and summed in bfloat16 or wider, within the bound.
A program may use at most 64 MiB of HBM per device.

v0:
```python
import math

import jax
import jax.numpy as jnp
from jax import lax
from jax.sharding import PartitionSpec as P

SECTIONS = 4


HIGH = lax.Precision.HIGHEST


def divide_complex(real_part, imag_part, denom_real, denom_imag):
    scale = denom_real * denom_real + denom_imag * denom_imag
    return (
        (real_part * denom_real + imag_part * denom_imag) / scale,
        (imag_part * denom_real - real_part * denom_imag) / scale,
    )


def modal_terms(omega, loss, freqs):
    stiff = omega * omega
    real_part = stiff[None, :] - (freqs * freqs)[:, None]
    imag_part = jnp.broadcast_to((loss * stiff)[None, :], real_part.shape)
    return (real_part, imag_part)


def couple_rows(shell_modes, wet_rows, node_rows, live_counts):
    depth, width, cavity = wet_rows.shape
    block = math.gcd(depth, 256)
    result = jnp.zeros((shell_modes.shape[1], cavity), jnp.float32)
    source = 0

    def add_block(number, carry, source=source):
        first = number * block
        piece = lax.dynamic_slice(wet_rows, (first, source, 0), (block, 1, cavity)).reshape(
            block, cavity
        )
        picks = lax.dynamic_slice(node_rows, (first, source), (block, 1)).reshape(block)
        shell_rows = shell_modes[picks]
        return carry + lax.dot_general(
            shell_rows, piece, (((0,), (0,)), ((), ())), preferred_element_type=jnp.float32
        )

    result = lax.fori_loop(0, (live_counts[source] + block - 1) // block, add_block, result)
    return result


def on_device(
    acoustic_modes,
    shell_modes,
    wet_counts,
    fluid_nodes,
    shell_nodes,
    wet_area,
    shell_freq,
    shell_loss,
    cavity_freq,
    cavity_loss,
    freqs,
    modal_force,
    cavity_source,
):
    groups = lax.axis_size("grp")
    member = lax.axis_index("grp")
    slots = fluid_nodes.shape[0]
    freq_total = freqs.shape[0]
    freq_count = freq_total // groups
    count = wet_counts[0]
    live = (jnp.arange(slots, dtype=jnp.int32) < count).astype(jnp.float32)
    wet_rows = (
        wet_area[:, None] * acoustic_modes[fluid_nodes].astype(jnp.float32) * live[:, None]
    ).astype(jnp.bfloat16)
    partial_sum = couple_rows(shell_modes, wet_rows[:, None, :], shell_nodes[:, None], [count])
    ds_re, ds_im = modal_terms(shell_freq, shell_loss, freqs)
    da_re, da_im = modal_terms(cavity_freq, cavity_loss, freqs)
    free_re, free_im = divide_complex(
        jnp.broadcast_to(cavity_source[None, :], da_re.shape), jnp.zeros_like(da_re), da_re, da_im
    )
    free_amps = jnp.concatenate([free_re, free_im], 0).astype(jnp.bfloat16)
    free_field = lax.dot_general(
        acoustic_modes, free_amps, (((1,), (1,)), ((), ())), preferred_element_type=jnp.float32
    )
    squared = (freqs * freqs)[:, None]
    coupling = lax.psum(partial_sum, ("fluid", "grp"))
    start = member * freq_count

    def own_rows(values):
        return lax.dynamic_slice_in_dim(values, start, freq_count, 0)

    shell_re, shell_im = (own_rows(ds_re), own_rows(ds_im))
    cavity_re, cavity_im = (own_rows(da_re), own_rows(da_im))
    base_re, base_im = (own_rows(free_re), own_rows(free_im))
    own_squared = own_rows(squared)
    coupled_re = jnp.zeros_like(base_re)
    coupled_im = jnp.zeros_like(base_im)
    for section in range(SECTIONS):
        amounts = jnp.concatenate([base_re + coupled_re, base_im + coupled_im], 0)
        loads = jnp.dot(amounts, coupling.T, precision=HIGH)
        struct_re, struct_im = divide_complex(
            modal_force[None, :] + loads[:freq_count], loads[freq_count:], shell_re, shell_im
        )
        back = jnp.dot(jnp.concatenate([struct_re, struct_im], 0), coupling, precision=HIGH)
        coupled_re, coupled_im = divide_complex(
            own_squared * back[:freq_count], own_squared * back[freq_count:], cavity_re, cavity_im
        )
    mine = jnp.stack([coupled_re, coupled_im]).astype(jnp.bfloat16)
    coupled_amps = lax.all_gather(mine, "grp", axis=1, tiled=True).reshape(2 * freq_total, -1)
    modal_structure = jnp.stack([struct_re, struct_im])
    coupled_field = lax.dot_general(
        acoustic_modes, coupled_amps, (((1,), (1,)), ((), ())), preferred_element_type=jnp.float32
    )
    pressure = (free_field + coupled_field).astype(jnp.bfloat16)
    return (pressure, modal_structure)


def solution(mesh):
    placed = (
        P(("fluid", "grp"), None),
        P("fluid", None),
        P(("fluid", "grp")),
        P(("fluid", "grp")),
        P(("fluid", "grp")),
        P(("fluid", "grp")),
        P(),
        P(),
        P(),
        P(),
        P(),
        P(),
        P(),
    )
    return jax.shard_map(
        on_device,
        mesh=mesh,
        in_specs=placed,
        out_specs=(P(("fluid", "grp"), None), P(None, "grp", None)),
        check_vma=False,
    )
```

profile of v0, /device:TPU:1, one launch (start us, length us, event | category | flops | bytes accessed | tf_op | source)
XLA Modules:
  0.0 339.2 jit_solution(15844099126047082016)
XLA Ops:
  7.2 0.0 all-reduce.2.cloned.1.call-start
  7.9 0.0 copy-start.6
  7.9 10.7 %copy.19 = bf16[8192,400]{1,0:T(8,128)(2,1)} copy(bf16[8192,400]{0,1:T(8,128)(2,1)} %param.15) | data formatting | bytes 13107200 | tf_op args[0]
  18.6 0.0 copy-done.6
  18.6 0.0 copy-start.4
  18.6 12.1 %gather_fusion.1 = bf16[2048,400]{1,0:T(8,128)(2,1)S(1)} fusion(bf16[8192,400]{1,0:T(8,128)(2,1)} %copy.19, s32[2048]{0:T(1024)S(1)} %fusion.69), kind=kCustom, calls=%fused_computation.1 | custom fusion | bytes 3284992 | tf_op jit(solution)/shard_map/gather | solution.py:73
  30.7 0.0 copy-done.4
  30.7 1.7 fusion.6
  32.4 2.8 copy.21
  35.2 1.4 copy.20
  36.7 0.0 copy-start.11
  36.7 0.0 copy-start.7
  36.7 0.0 copy-start.8
  36.7 0.0 copy-start.5
  36.7 13.1 %while.10 = (s32[]{:T(128)}, f32[300,400]{0,1:T(8,128)S(1)}, s32[]{:T(128)}, s32[2048,1]{0,1:T(1,128)}, bf16[1024,300]{1,0:T(8,128)(2,1)S(1)}, /*index=5*/bf16[2...) while((s32[]{:T(128)}, f32[300,400]{0,1:T(8,128)S(1)}, s32[]{:T(128)}, ...), condition=%wide.region_1.2_spmd, body=%wide.region_0.1_spmd.sunk | while | flops 61561796 | bytes 1811355 | solution.py:46
  36.8 0.7 compare_select_fusion.3
  37.5 1.2 gather_fusion
  38.6 0.3 convolution_add_fusion.3
  39.0 0.7 compare_select_fusion.3
  39.7 1.2 gather_fusion
  40.8 0.3 convolution_add_fusion.3
  41.2 0.7 compare_select_fusion.3
  41.8 1.2 gather_fusion
  43.0 0.3 convolution_add_fusion.3
  43.3 0.7 compare_select_fusion.3
  44.0 1.2 gather_fusion
  45.2 0.3 convolution_add_fusion.3
  45.5 0.7 compare_select_fusion.3
  46.2 1.2 gather_fusion
  47.4 0.3 convolution_add_fusion.3
  47.7 0.7 compare_select_fusion.3
  48.4 1.2 gather_fusion
  49.6 0.3 convolution_add_fusion.3
  49.9 0.0 copy-start.1
  49.9 0.8 copy-done.1
  50.7 0.0 all-reduce.2.cloned.1.call-update
  50.8 0.0 copy-done.11
  50.8 0.1 fusion.8
  51.0 0.0 copy-start.9
  51.0 0.0 copy-start.10
  51.0 0.0 copy-start.3
  51.0 6.2 %fusion.12 = f32[128,8192]{1,0:T(8,128)} fusion(bf16[8192,400]{0,1:T(8,128)(2,1)} %param.15, bf16[64,400]{1,0:T(8,128)(2,1)S(1)} %get-tuple-element.88, bf16[64,400]{1,0:T(8,128)(2,1)S(1)} %get-tuple-element.85), kind=kOutput, calls=%fused_computation.22 | convolution fusion | flops 839065600 | bytes 10850304 | tf_op jit(solution)/shard_map/dot_general | solution.py:82
  57.2 0.1 dynamic-slice.5
  57.2 250.6 %all-reduce.2.cloned.1.call-done = f32[300,400]{0,1:T(8,128)} async-done(((f32[300,400]{0,1:T(8,128)}), f32[300,400]{0,1:T(8,128)}) %all-reduce.2.cloned.1.call-update) | async-done | bytes 480016 | tf_op jit(solution)/shard_map/psum | solution.py:86
  307.9 1.7 fusion.16
  309.5 0.1 fusion.51
  309.6 1.8 fusion.32
  311.4 0.1 divide_add_fusion.5
  311.5 1.5 fusion.20
  313.0 0.1 fusion.57
  313.1 1.8 fusion.36
  314.8 0.1 divide_add_fusion.3
  314.9 1.5 fusion.24
  316.4 0.1 fusion.55
  316.5 0.7 fusion.40
  317.2 0.1 divide_add_fusion.1
  317.3 0.4 fusion.28
  317.8 0.1 fusion.53
  317.9 0.7 fusion.44
  318.6 0.1 fusion.66
  318.7 6.5 %all_gather.3 = bf16[2,64,400]{2,1,0:T(8,128)(2,1)S(1)} all-gather(bf16[2,16,400]{2,1,0:T(8,128)(2,1)S(1)} %pad_maximum_fusion.1), channel_id=1, replica_groups=mesh['fluid'=64,'grp'=4] {'grp'}, dimensions={1}, use_global_device_ids=true | all-gather | bytes 128000 | tf_op jit(solution)/shard_map/all_gather | solution.py:109
  325.1 4.1 %fusion.4 = bf16[8192,128]{0,1:T(8,128)(2,1)S(1)} fusion(f32[128,8192]{1,0:T(8,128)S(1)} %copy-done.2, bf16[128,400]{1,0:T(8,128)(2,1)S(1)} %bitcast.38, bf16[8192,400]{0,1:T(8,128)(2,1)} %param.15), kind=kOutput, calls=%fused_computation.10 | convolution fusion | flops 840957952 | bytes 12947456 | tf_op jit(solution)/shard_map/dot_general | solution.py:111
  329.3 2.4 copy.22
  331.7 0.6 pad_maximum_fusion
  (25 shorter events, 0.2 us)
Async XLA Ops:
  7.2 300.7 %all-reduce.2.cloned.1.call-start = ((), (), s32[]{:S(2)}) async-start(), calls=%async_computation | async-start | bytes 1228800 | tf_op jit(solution)/shard_map/psum | solution.py:86
  7.9 10.7 %copy-start.6 = (s32[2048]{0:T(1024)S(1)}, s32[2048]{0:T(1024)}, u32[]{:S(2)}) copy-start(s32[2048]{0:T(1024)} %param.18) | copy-start | bytes 24580
  18.6 12.1 %copy-start.4 = (f32[2048]{0:T(1024)S(1)}, f32[2048]{0:T(1024)}, u32[]{:S(2)}) copy-start(f32[2048]{0:T(1024)} %param.20) | copy-start | bytes 24580
  36.7 14.1 %copy-start.11 = (f32[64]{0:T(128)S(1)}, f32[64]{0:T(128)}, u32[]{:S(2)}) copy-start(f32[64]{0:T(128)} %param.25) | copy-start | bytes 772
  36.7 14.1 %copy-start.7 = (f32[400]{0:T(512)S(1)}, f32[400]{0:T(512)}, u32[]{:S(2)}) copy-start(f32[400]{0:T(512)} %param.24) | copy-start | bytes 4804
  36.7 14.1 %copy-start.8 = (f32[400]{0:T(512)S(1)}, f32[400]{0:T(512)}, u32[]{:S(2)}) copy-start(f32[400]{0:T(512)} %param.23) | copy-start | bytes 4804
  36.7 14.1 %copy-start.5 = (f32[400]{0:T(512)S(1)}, f32[400]{0:T(512)}, u32[]{:S(2)}) copy-start(f32[400]{0:T(512)} %param.27) | copy-start | bytes 4804
  49.9 0.8 copy-start.1
  51.0 6.3 %copy-start.9 = (f32[300]{0:T(512)S(1)}, f32[300]{0:T(512)}, u32[]{:S(2)}) copy-start(f32[300]{0:T(512)} %param.22) | copy-start | bytes 3604
  51.0 6.3 %copy-start.10 = (f32[300]{0:T(512)S(1)}, f32[300]{0:T(512)}, u32[]{:S(2)}) copy-start(f32[300]{0:T(512)} %param.21) | copy-start | bytes 3604
  51.0 258.5 %copy-start.3 = (f32[300]{0:T(512)S(1)}, f32[300]{0:T(512)}, u32[]{:S(2)}) copy-start(f32[300]{0:T(512)} %param.26) | copy-start | bytes 3604
  307.9 8.7 %copy-start = (f32[300,400]{0,1:T(8,128)S(1)}, f32[300,400]{0,1:T(8,128)}, u32[]{:S(2)}) copy-start(f32[300,400]{0,1:T(8,128)} %all-reduce.2.cloned.1.call-done) | copy-start | bytes 1440004
  307.9 17.3 %copy-start.2 = (f32[128,8192]{1,0:T(8,128)S(1)}, f32[128,8192]{1,0:T(8,128)}, u32[]{:S(2)}) copy-start(f32[128,8192]{1,0:T(8,128)} %fusion.12) | copy-start | bytes 12582916
Sparse Core Ops, SparseCore 0:
  50.9 256.9 all-reduce.1
where the time goes:
time: 340 us; the launch traced here: 339 us
  waiting for transfers between devices  251 us (74%)
  local copies, waits for them, and re-layouts  37.4 us (11%)
  matrix products  22 us (6%)
  between operations  15 us (4%)
  other arithmetic  7.34 us (2%)
  blocking collectives  6.48 us (2%)
    psum x1, waiting for transfers between devices, on_device(): coupling = lax.psum(partial_sum, ('fluid', 'grp'))  251 us
    unnamed x26, local copies, waits for them, and re-layouts  14 us
    gather x1, local copies, waits for them, and re-layouts, on_device(): acoustic_modes[fluid_nodes].astype(jnp.float32)  12.1 us
    gather x6, local copies, waits for them, and re-layouts, add_block(): shell_rows = shell_modes[picks]  6.98 us
  transfers between devices with their start and end apart: 1, of which 1 were waited for; matrix products, arithmetic and copies ran while one was open for 2% of the time, Pallas kernels for 0%

commit v1 on v0

v1 whole, which is shorter than its diff:
```python
import functools

import jax
import jax.numpy as jnp
from jax import lax
from jax.experimental import pallas as pl
from jax.experimental.pallas import tpu as pltpu
from jax.sharding import PartitionSpec as P

SECTIONS = 4
MESH = pl.DeviceIdType.MESH
LANES = 128
DIGITS = (("z", 8), ("xh", 2), ("y", 4), ("xl", 2), ("c", 2))
PLANE = ("xh", "y", "xl")
STACK = ("z", "c")


def sizes_of(names):
    table = dict(DIGITS)
    return [table[name] for name in names]


def offsets_of(names):
    places = [()]
    for size in sizes_of(names):
        places = [place + (step,) for place in places for step in range(size)]
    return places[1:]


def own_digits():
    fluid, grp = lax.axis_index("fluid"), lax.axis_index("grp")
    return {
        "z": fluid // 8,
        "xh": (fluid // 4) % 2,
        "y": fluid % 4,
        "xl": grp // 2,
        "c": grp % 2,
    }


def moved(digits, names, offset):
    there = dict(digits)
    for name, size, step in zip(names, sizes_of(names), offset):
        there[name] = lax.rem(digits[name] + step, size)
    return there


def place_of(digits):
    return (digits["z"] * 8 + digits["xh"] * 4 + digits["y"], digits["xl"] * 2 + digits["c"])


def rank_of(digits, names):
    rank = 0
    for name, size in zip(names, sizes_of(names)):
        rank = rank * size + digits[name]
    return rank


def gather_kernel(modes_ref, shell_ref, fluid_ref, node_ref, weight_ref, out_ref, wet_ref, pick_ref):
    step = pl.program_id(0)
    depth = modes_ref.shape[1]
    slots = fluid_ref.shape[1]
    block = 256

    def one_hot(rows, base, picks):
        number = lax.broadcasted_iota(jnp.int32, (rows, picks.shape[1]), 0) + base
        return jnp.where(number == picks, 1.0, 0.0).astype(jnp.bfloat16)

    @pl.when(step == 0)
    def _():
        for first in range(0, slots, block):
            span = pl.ds(first, block)
            hot = one_hot(shell_ref.shape[1], 0, node_ref[:, span])
            pick_ref[:, span] = jnp.dot(
                shell_ref[...], hot, preferred_element_type=jnp.float32
            ).astype(jnp.bfloat16)

    for first in range(0, slots, block):
        span = pl.ds(first, block)
        hot = one_hot(depth, step * depth, fluid_ref[:, span])
        part = jnp.dot(modes_ref[...], hot, preferred_element_type=jnp.float32)

        @pl.when(step == 0)
        def _():
            wet_ref[:, span] = part

        @pl.when(step > 0)
        def _():
            wet_ref[:, span] += part

    @pl.when(step == pl.num_programs(0) - 1)
    def _():
        wet = (wet_ref[...] * weight_ref[...]).astype(jnp.bfloat16)
        total = lax.dot_general(
            wet, pick_ref[...], (((1,), (1,)), ((), ())), preferred_element_type=jnp.float32
        )
        rows = total.shape[0]
        columns = total.shape[1]
        total = jnp.concatenate(
            [total, jnp.zeros((rows, -columns % LANES), jnp.float32)], 1
        ).astype(jnp.bfloat16)
        for part in range(total.shape[1] // LANES):
            out_ref[pl.ds(part * rows, rows), :] = total[:, part * LANES : (part + 1) * LANES]
        used = rows * (total.shape[1] // LANES)
        out_ref[pl.ds(used, out_ref.shape[0] - used), :] = jnp.zeros(
            (out_ref.shape[0] - used, LANES), jnp.bfloat16
        )


def partial_coupling(modes, shell, fluid_nodes, shell_nodes, weights, rows):
    cavity, depth = modes.shape
    slots = fluid_nodes.shape[1]
    chunk = 1024
    whole = lambda shape: pl.BlockSpec(shape, lambda k: (0, 0))
    return pl.pallas_call(
        gather_kernel,
        grid=(depth // chunk,),
        in_specs=[
            pl.BlockSpec((cavity, chunk), lambda k: (0, k)),
            whole(shell.shape),
            whole((1, slots)),
            whole((1, slots)),
            whole((1, slots)),
        ],
        out_specs=whole((rows, LANES)),
        out_shape=jax.ShapeDtypeStruct((rows, LANES), jnp.bfloat16),
        scratch_shapes=[
            pltpu.VMEM((cavity, slots), jnp.float32),
            pltpu.VMEM((shell.shape[0], slots), jnp.bfloat16),
        ],
        compiler_params=pltpu.CompilerParams(
            dimension_semantics=("arbitrary",), vmem_limit_bytes=48 << 20
        ),
    )(modes, shell, fluid_nodes, shell_nodes, weights)


def column_of(row):
    size = row.shape[1]
    below = lax.broadcasted_iota(jnp.int32, (size, size), 0)
    across = lax.broadcasted_iota(jnp.int32, (size, size), 1)
    spread = jnp.where(below == across, jnp.broadcast_to(row, (size, size)), 0.0)
    return jnp.sum(spread, axis=1, keepdims=True)


def inverse_terms(omega, loss, squared):
    stiff = omega * omega
    real_part = stiff - squared
    imag_part = jnp.broadcast_to(loss * stiff, real_part.shape)
    scale = real_part * real_part + imag_part * imag_part
    return real_part / scale, imag_part / scale


def solve_kernel(
    part_ref,
    shell_freq_ref,
    shell_loss_ref,
    cavity_freq_ref,
    cavity_loss_ref,
    freqs_ref,
    force_ref,
    source_ref,
    amps_ref,
    structure_ref,
    plane_ref,
    mine_ref,
    stack_ref,
    full_ref,
    send_sem,
    recv_sem,
):
    digits = own_digits()
    plane, stack = offsets_of(PLANE), offsets_of(STACK)
    size = mine_ref.shape[0]
    barrier = pltpu.get_barrier_semaphore()
    for names, offsets in ((PLANE, plane), (STACK, stack)):
        for offset in offsets:
            pl.semaphore_signal(
                barrier,
                inc=1,
                device_id=place_of(moved(digits, names, offset)),
                device_id_type=MESH,
            )
    pl.semaphore_wait(barrier, len(plane) + len(stack))

    def rows_of(rank):
        return pl.ds(pl.multiple_of(rank * size, size), size)

    for slot, offset in enumerate(plane):
        there = moved(digits, PLANE, offset)
        pltpu.make_async_remote_copy(
            src_ref=part_ref.at[rows_of(rank_of(there, PLANE))],
            dst_ref=plane_ref.at[slot],
            send_sem=send_sem.at[0],
            recv_sem=recv_sem.at[0],
            device_id=place_of(there),
            device_id_type=MESH,
        ).start()

    frequencies = column_of(freqs_ref[...])
    squared = frequencies * frequencies
    shell_p, shell_q = inverse_terms(shell_freq_ref[...], shell_loss_ref[...], squared)
    cavity_p, cavity_q = inverse_terms(cavity_freq_ref[...], cavity_loss_ref[...], squared)
    base_re = source_ref[...] * cavity_p
    base_im = -source_ref[...] * cavity_q
    back_p, back_q = squared * cavity_p, squared * cavity_q

    pltpu.make_async_copy(plane_ref, plane_ref, recv_sem.at[0]).wait()
    own = rank_of(digits, PLANE)
    mine_ref[...] = (
        part_ref[rows_of(own), :].astype(jnp.float32)
        + jnp.sum(plane_ref[...].astype(jnp.float32), axis=0)
    ).astype(jnp.bfloat16)

    for slot, offset in enumerate(stack):
        pltpu.make_async_remote_copy(
            src_ref=mine_ref,
            dst_ref=stack_ref.at[slot],
            send_sem=send_sem.at[1],
            recv_sem=recv_sem.at[1],
            device_id=place_of(moved(digits, STACK, offset)),
            device_id_type=MESH,
        ).start()
    pltpu.make_async_copy(stack_ref, stack_ref, recv_sem.at[1]).wait()
    full_ref[rows_of(own), :] = (
        mine_ref[...].astype(jnp.float32)
        + jnp.sum(stack_ref[...].astype(jnp.float32), axis=0)
    ).astype(jnp.bfloat16)

    for offset in plane:
        pltpu.make_async_remote_copy(
            src_ref=full_ref.at[rows_of(own)],
            dst_ref=full_ref.at[rows_of(own)],
            send_sem=send_sem.at[2],
            recv_sem=recv_sem.at[2],
            device_id=place_of(moved(digits, PLANE, offset)),
            device_id_type=MESH,
        ).start()
    pltpu.make_async_copy(plane_ref, plane_ref, recv_sem.at[2]).wait()

    cavity = base_re.shape[1]
    shells = shell_p.shape[1]
    count = squared.shape[0]
    coupling = jnp.concatenate(
        [full_ref[pl.ds(at * cavity, cavity), :] for at in range(pl.cdiv(shells, LANES))], 1
    )[:, :shells]
    force = force_ref[...]
    real, imag = base_re, base_im
    for section in range(SECTIONS):
        loads = jnp.dot(
            jnp.concatenate([real, imag], 0).astype(jnp.bfloat16),
            coupling,
            preferred_element_type=jnp.float32,
        )
        load_re, load_im = force + loads[:count], loads[count:]
        struct_re = load_re * shell_p + load_im * shell_q
        struct_im = load_im * shell_p - load_re * shell_q
        back = lax.dot_general(
            jnp.concatenate([struct_re, struct_im], 0).astype(jnp.bfloat16),
            coupling,
            (((1,), (1,)), ((), ())),
            preferred_element_type=jnp.float32,
        )
        back_re, back_im = back[:count], back[count:]
        real = base_re + (back_re * back_p + back_im * back_q)
        imag = base_im + (back_im * back_p - back_re * back_q)
    amps_ref[...] = jnp.concatenate([real, imag], 0).astype(jnp.bfloat16)
    structure_ref[0] = struct_re
    structure_ref[1] = struct_im

    pltpu.make_async_copy(plane_ref, plane_ref, send_sem.at[0]).wait()
    pltpu.make_async_copy(stack_ref, stack_ref, send_sem.at[1]).wait()
    pltpu.make_async_copy(plane_ref, plane_ref, send_sem.at[2]).wait()


def solve(part, terms, count, shells, cavity):
    planes, stacks = len(offsets_of(PLANE)), len(offsets_of(STACK))
    size = part.shape[0] // (planes + 1)
    inside = pl.BlockSpec(memory_space=pltpu.VMEM)
    return pl.pallas_call(
        solve_kernel,
        in_specs=[inside] * (1 + len(terms)),
        out_specs=[inside] * 2,
        out_shape=[
            jax.ShapeDtypeStruct((2 * count, cavity), jnp.bfloat16),
            jax.ShapeDtypeStruct((2, count, shells), jnp.float32),
        ],
        scratch_shapes=[
            pltpu.VMEM((planes, size, LANES), jnp.bfloat16),
            pltpu.VMEM((size, LANES), jnp.bfloat16),
            pltpu.VMEM((stacks, size, LANES), jnp.bfloat16),
            pltpu.VMEM(part.shape, jnp.bfloat16),
            pltpu.SemaphoreType.DMA((3,)),
            pltpu.SemaphoreType.DMA((3,)),
        ],
        compiler_params=pltpu.CompilerParams(
            collective_id=0, has_side_effects=True, vmem_limit_bytes=32 << 20
        ),
    )(part, *terms)


def field_kernel(amps_ref, modes_ref, structure_ref, pressure_ref, own_ref):
    field = jnp.dot(amps_ref[...], modes_ref[...], preferred_element_type=jnp.float32)
    pressure_ref[...] = field.T.astype(jnp.bfloat16)

    @pl.when(pl.program_id(0) == 0)
    def _():
        count = own_ref.shape[1]
        first = pl.multiple_of(lax.axis_index("grp") * count, count)
        own_ref[...] = structure_ref[:, pl.ds(first, count), :]


def field(amps, modes, structure, groups):
    cavity, depth = modes.shape
    chunk = 1024
    parts, count, shells = structure.shape
    own = (parts, count // groups, shells)
    return pl.pallas_call(
        field_kernel,
        grid=(depth // chunk,),
        in_specs=[
            pl.BlockSpec(amps.shape, lambda k: (0, 0)),
            pl.BlockSpec((cavity, chunk), lambda k: (0, k)),
            pl.BlockSpec(structure.shape, lambda k: (0, 0, 0)),
        ],
        out_specs=[
            pl.BlockSpec((chunk, amps.shape[0]), lambda k: (k, 0)),
            pl.BlockSpec(own, lambda k: (0, 0, 0)),
        ],
        out_shape=[
            jax.ShapeDtypeStruct((depth, amps.shape[0]), jnp.bfloat16),
            jax.ShapeDtypeStruct(own, jnp.float32),
        ],
        compiler_params=pltpu.CompilerParams(dimension_semantics=("arbitrary",)),
    )(amps, modes, structure)


def on_device(
    acoustic_modes,
    shell_modes,
    wet_counts,
    fluid_nodes,
    shell_nodes,
    wet_area,
    shell_freq,
    shell_loss,
    cavity_freq,
    cavity_loss,
    freqs,
    modal_force,
    cavity_source,
):
    groups = lax.axis_size("grp")
    slots = fluid_nodes.shape[0]
    live = jnp.arange(slots, dtype=jnp.int32) < wet_counts[0]
    weights = jnp.where(live, wet_area, 0.0)
    modes = acoustic_modes.T
    shells, cavity = shell_modes.shape[1], acoustic_modes.shape[1]
    unit = 16 * (len(offsets_of(PLANE)) + 1)
    rows = pl.cdiv(cavity * pl.cdiv(shells, LANES), unit) * unit
    part = partial_coupling(
        modes,
        shell_modes.T,
        fluid_nodes[None, :],
        shell_nodes[None, :],
        weights[None, :],
        rows,
    )
    terms = (shell_freq, shell_loss, cavity_freq, cavity_loss, freqs, modal_force, cavity_source)
    amps, structure = solve(
        part, [term[None, :] for term in terms], freqs.shape[0], shells, cavity
    )
    return tuple(field(amps, modes, structure, groups))


def solution(mesh):
    both = P(("fluid", "grp"))
    placed = (P(("fluid", "grp"), None), P("fluid", None)) + (both,) * 4 + (P(),) * 7
    return jax.shard_map(
        on_device,
        mesh=mesh,
        in_specs=placed,
        out_specs=(P(("fluid", "grp"), None), P(None, "grp", None)),
        check_vma=False,
    )
```

time: 340 us -> 94.6 us (0.28)
  waiting for transfers between devices: 251 us -> 0 us
  Pallas kernels: 0 us -> 86.2 us
  local copies, waits for them, and re-layouts: 37.4 us -> 5.84 us
  matrix products: 22 us -> 0 us
  between operations: 15 us -> 1.4 us
  other arithmetic: 7.34 us -> 0.7 us
  blocking collectives: 6.48 us -> 0 us
    psum x1 -> x0, waiting for transfers between devices: 251 us -> none  [on_device(): coupling = lax.psum(partial_sum, ('fluid', 'grp'))]
    pallas_call x0 -> x3, Pallas kernels: none -> 86.2 us  [the longest x1 43.5 us: partial_coupling(): pl.pallas_call(gather_kernel, grid=(depth // chunk,), in_specs=[pl.BlockS...]
    dot_general x16 -> x0, matrix products: 22 us -> none  [the longest x1 6.15 us: on_device(): lax.dot_general(acoustic_modes, free_amps, (((1,), (1,)), ((), ())), pref...]
    gather x7 -> x0, local copies, waits for them, and re-layouts: 19 us -> none  [the longest x1 12.1 us: on_device(): acoustic_modes[fluid_nodes].astype(jnp.float32)]
    unnamed x26 -> x18, local copies, waits for them, and re-layouts: 14 us -> 3.79 us
    all_gather x1 -> x0, blocking collectives: 6.48 us -> none  [on_device(): lax.all_gather(mine, 'grp', axis=1, tiled=True).reshape(2 * freq_total, -1)]
    while x2 -> x0, local copies, waits for them, and re-layouts: 4.22 us -> none  [couple_rows(): lax.fori_loop(0, (live_counts[source] + block - 1) // block, add_block, r...]
    select_n x6 -> x1, other arithmetic: 4.12 us -> 0.7 us  [on_device(): weights = jnp.where(live, wet_area, 0.0)]
  transfers between devices with their start and end apart: 1 -> 0, of which waited for: 1 -> 0; matrix products, arithmetic and copies ran while one was open for 2% -> 0% of each run, Pallas kernels for 0% -> 0%
where the time goes in v1:
time: 94.6 us; the launch traced here: 94.1 us
  Pallas kernels  86.2 us (91%)
  local copies, waits for them, and re-layouts  5.84 us (6%)
  between operations  1.4 us (1%)
    pallas_call x1, Pallas kernels, partial_coupling(): pl.pallas_call(gather_kernel, grid=(depth // chunk,), in_specs=[pl.BlockS...  43.5 us
    pallas_call x1, Pallas kernels, solve(): pl.pallas_call(solve_kernel, in_specs=[inside] * (1 + len(terms)), out_sp...  34.6 us
    pallas_call x1, Pallas kernels, field(): pl.pallas_call(field_kernel, grid=(depth // chunk,), in_specs=[pl.BlockSp...  8.03 us
    unnamed x18, local copies, waits for them, and re-layouts  3.79 us
    broadcast_in_dim x3, local copies, waits for them, and re-layouts, on_device(): term[None, :]  2.05 us

profile of v1, /device:TPU:1, one launch (start us, length us, event | category | flops | bytes accessed | tf_op | source)
XLA Modules:
  0.0 94.1 jit_solution(8513462097636887867)
XLA Ops:
  0.6 0.0 copy-start.7
  0.6 0.0 copy-start.8
  0.7 0.0 copy-start.6
  0.7 0.0 copy-start.5
  1.3 0.7 broadcast_in_dim.38.shell_freq_ref
  2.0 0.7 broadcast_in_dim.39.shell_loss_ref
  2.7 0.7 broadcast_in_dim.43.force_ref
  3.4 0.7 fusion
  4.1 0.0 copy-start
  4.1 1.1 %copy-done = bf16[1024,300]{0,1:T(8,128)(2,1)S(1)} copy-done((bf16[1024,300]{0,1:T(8,128)(2,1)S(1)}, bf16[1024,300]{0,1:T(8,128)(2,1)}, u32[]{:S(2)}) %copy-start) | copy-done | bytes 614424
  5.2 0.0 copy-start.3
  5.2 0.7 copy-done.3
  5.9 0.0 copy-start.4
  5.9 0.7 copy-done.4
  6.6 43.5 %shard_map.140.part_ref = bf16[1280,128]{1,0:T(8,128)(2,1)S(1)} custom-call(bf16[400,8192]{1,0:T(8,128)(2,1)} %bitcast.19, bf16[300,1024]{1,0:T(8,128)(2,1)S(1)} %bitcast.11, s32[1,2048]{1,0:T(1,128)S(1)} %bitcast.13, s32[1,2048]{1,0:T(1,128)S(1)} %bitcast.14, f32[1,2048]{1,0:T(1,128)S(1)} %bitcast.12), custom_call_target="tpu_custom_call" | custom-call | tf_op jit(solution)/shard_map/pallas_call | solution.py:115
  50.1 0.0 copy-done.7
  50.1 0.0 copy-done.8
  50.1 0.0 copy-done.6
  50.1 0.0 copy-done.5
  50.1 34.6 %shard_map.141 = (bf16[128,400]{1,0:T(8,128)(2,1)S(1)}, f32[2,64,300]{2,1,0:T(8,128)S(1)}) custom-call(bf16[1280,128]{1,0:T(8,128)(2,1)S(1)} %shard_map.140.part_ref, f32[1,300]{1,0:T(1,128)S(1)} %broadcast_in_dim.38.shell_freq_ref, f32[1,300]{1,0:T(1,128)S(1)} %broadcast_in_dim.39.shell_loss_ref, f32[1,400]{1,0:T(1,128)S(1)} %bitcast.15, ...), custom_call_target="tpu_custom_call" | custom-call | tf_op jit(solution)/shard_map/pallas_call | solution.py:279
  84.8 0.0 copy-start.1
  84.8 0.7 copy-done.1
  85.4 0.0 copy-start.2
  85.4 0.6 copy-done.2
  86.1 8.0 %shard_map.142 = (bf16[8192,128]{1,0:T(8,128)(2,1)}, f32[2,16,300]{2,1,0:T(8,128)}) custom-call(bf16[128,400]{1,0:T(8,128)(2,1)} %copy-done.2, bf16[400,8192]{1,0:T(8,128)(2,1)} %bitcast.20, f32[2,64,300]{2,1,0:T(8,128)} %copy-done.1), custom_call_target="tpu_custom_call" | custom-call | tf_op jit(solution)/shard_map/pallas_call | solution.py:317
Async XLA Ops:
  0.6 49.4 %copy-start.7 = (f32[400]{0:T(512)S(1)}, f32[400]{0:T(512)}, u32[]{:S(2)}) copy-start(f32[400]{0:T(512)} %param.25) | copy-start | bytes 4804
  0.6 49.4 %copy-start.8 = (f32[64]{0:T(128)S(1)}, f32[64]{0:T(128)}, u32[]{:S(2)}) copy-start(f32[64]{0:T(128)} %param.23) | copy-start | bytes 772
  0.7 49.4 %copy-start.6 = (f32[400]{0:T(512)S(1)}, f32[400]{0:T(512)}, u32[]{:S(2)}) copy-start(f32[400]{0:T(512)} %param.22) | copy-start | bytes 4804
  0.7 49.4 %copy-start.5 = (f32[400]{0:T(512)S(1)}, f32[400]{0:T(512)}, u32[]{:S(2)}) copy-start(f32[400]{0:T(512)} %param.21) | copy-start | bytes 4804
  4.1 1.1 %copy-start = (bf16[1024,300]{0,1:T(8,128)(2,1)S(1)}, bf16[1024,300]{0,1:T(8,128)(2,1)}, u32[]{:S(2)}) copy-start(bf16[1024,300]{0,1:T(8,128)(2,1)} %param.14) | copy-start | bytes 1843204
  5.2 0.7 copy-start.3
  5.9 0.7 copy-start.4
  84.8 0.7 copy-start.1
  85.4 0.6 copy-start.2

commit v2 on v1

v2 whole, which is shorter than its diff:
```python
import jax
import jax.numpy as jnp
from jax import lax
from jax.experimental import pallas as pl
from jax.experimental.pallas import tpu as pltpu
from jax.sharding import PartitionSpec as P

SECTIONS = 4
MESH = pl.DeviceIdType.MESH
LANES = 128
SIZES = {"z": 8, "xh": 2, "y": 4, "xl": 2, "c": 2}
PLANE = ("xh", "y", "xl", "c")
STACK = ("z",)
CHUNKS = 8
TAIL = 4


def offsets_of(names):
    places = [()]
    for name in names:
        places = [place + (step,) for place in places for step in range(SIZES[name])]
    return places[1:]


def own_digits():
    fluid, grp = lax.axis_index("fluid"), lax.axis_index("grp")
    return {
        "z": fluid // 8,
        "xh": (fluid // 4) % 2,
        "y": fluid % 4,
        "xl": grp // 2,
        "c": grp % 2,
    }


def moved(digits, names, offset):
    there = dict(digits)
    for name, step in zip(names, offset):
        if step:
            there[name] = lax.rem(digits[name] + step, SIZES[name])
    return there


def place_of(digits):
    return (digits["z"] * 8 + digits["xh"] * 4 + digits["y"], digits["xl"] * 2 + digits["c"])


def rank_of(digits, names):
    rank = 0
    for name in names:
        rank = rank * SIZES[name] + digits[name]
    return rank


def column_of(row):
    size = row.shape[1]
    below = lax.broadcasted_iota(jnp.int32, (size, size), 0)
    across = lax.broadcasted_iota(jnp.int32, (size, size), 1)
    spread = jnp.where(below == across, jnp.broadcast_to(row, (size, size)), 0.0)
    return jnp.sum(spread, axis=1, keepdims=True)


def inverse_terms(omega, loss, squared):
    stiff = omega * omega
    real_part = stiff - squared
    imag_part = jnp.broadcast_to(loss * stiff, real_part.shape)
    scale = real_part * real_part + imag_part * imag_part
    return real_part / scale, imag_part / scale


def pad_lanes(values, width):
    if values.shape[1] == width:
        return values
    rest = jnp.zeros((values.shape[0], width - values.shape[1]), values.dtype)
    return jnp.concatenate([values, rest], 1)


def pad_rows(values, height):
    if values.shape[0] == height:
        return values
    rest = jnp.zeros((height - values.shape[0], values.shape[1]), values.dtype)
    return jnp.concatenate([values, rest], 0)


def tail_height(shells):
    return pl.cdiv(pl.cdiv(shells, TAIL), 16) * 16


def rows_needed(shells, cavity, parts):
    high = pl.cdiv(shells, 16) * 16
    used = high * (cavity // LANES) + tail_height(shells)
    return pl.cdiv(used, 16 * parts) * 16 * parts


def pack(total, out_ref):
    shells, cavity = total.shape
    high = pl.cdiv(shells, 16) * 16
    full = cavity // LANES
    for at in range(full):
        piece = pad_rows(total[:, at * LANES : (at + 1) * LANES], high)
        out_ref[pl.ds(at * high, high), :] = piece.astype(out_ref.dtype)
    tall, wide = tail_height(shells), LANES // TAIL
    rest = pad_lanes(pad_rows(total[:, full * LANES :], tall * TAIL), wide)
    tail = jnp.concatenate([rest[at * tall : (at + 1) * tall] for at in range(TAIL)], 1)
    height = out_ref.shape[0] - full * high
    out_ref[pl.ds(full * high, height), :] = pad_rows(tail, height).astype(out_ref.dtype)


def unpack(full_ref, shells, cavity):
    high = pl.cdiv(shells, 16) * 16
    full = cavity // LANES
    tall, wide = tail_height(shells), LANES // TAIL
    blocks = [full_ref[pl.ds(at * high, high), :] for at in range(full)]
    tail = full_ref[pl.ds(full * high, tall), :].astype(jnp.float32)
    rest = [tail[:, at * wide : at * wide + cavity - full * LANES] for at in range(TAIL)]
    rest = jnp.concatenate(rest, 0)[:high].astype(full_ref.dtype)
    return jnp.concatenate(blocks + [rest], 1)[:shells]


def outer(value):
    return pltpu.with_memory_space_constraint(value, pltpu.HBM)


def gather_kernel(
    modes_hbm,
    shell_hbm,
    count_ref,
    fluid_hbm,
    node_hbm,
    area_hbm,
    part_ref,
    modes_ref,
    shell_ref,
    fluid_ref,
    node_ref,
    area_ref,
    table_ref,
    rows_ref,
    pick_ref,
    area_rows_ref,
    modes_sem,
    small_sem,
):
    cavity, depth = modes_ref.shape
    shells, shell_depth = shell_ref.shape
    slots = fluid_ref.shape[0]
    chunk, span = depth // CHUNKS, slots // CHUNKS
    lane_blocks = pl.cdiv(cavity, LANES)

    pairs = [
        (shell_hbm, shell_ref),
        (node_hbm, node_ref),
        (area_hbm, area_ref),
        (fluid_hbm, fluid_ref),
    ]
    small = [
        pltpu.make_async_copy(source, target, small_sem.at[at])
        for at, (source, target) in enumerate(pairs)
    ]
    large = [
        pltpu.make_async_copy(
            modes_hbm.at[:, pl.ds(at * chunk, chunk)],
            modes_ref.at[:, pl.ds(at * chunk, chunk)],
            modes_sem.at[at],
        )
        for at in range(CHUNKS)
    ]
    for copy in small + large:
        copy.start()
    for copy in small:
        copy.wait()
    count = count_ref[0]
    for at in range(CHUNKS):
        here = pl.ds(at * span, span)
        slot = lax.broadcasted_iota(jnp.int32, (1, span), 1) + at * span
        node = jnp.where(slot < count, node_ref[here].reshape(1, span), -1)
        number = lax.broadcasted_iota(jnp.int32, (shell_depth, span), 0)
        hot = jnp.where(number == node, 1.0, 0.0).astype(jnp.bfloat16)
        pick_ref[:, here] = jnp.dot(
            shell_ref[...], hot, preferred_element_type=jnp.float32
        ).astype(jnp.bfloat16)
        area = area_ref[here].reshape(1, span)
        area_rows_ref[here, :] = jnp.broadcast_to(area, (LANES, span)).T
        large[at].wait()
        for block in range(lane_blocks):
            first = block * LANES
            wide = min(LANES, cavity - first)
            piece = modes_ref[first : first + wide, at * chunk : (at + 1) * chunk].T
            table_ref[pl.ds(at * chunk * lane_blocks + block, chunk, stride=lane_blocks), :] = (
                pad_lanes(piece.astype(jnp.float32), LANES)
            )

    unroll = 16

    def gather(step, carry):
        for at in range(unroll):
            slot = step * unroll + at
            first = pl.multiple_of(fluid_ref[slot] * lane_blocks, lane_blocks)
            rows_ref[pl.ds(pl.multiple_of(slot * lane_blocks, lane_blocks), lane_blocks), :] = (
                table_ref[pl.ds(first, lane_blocks), :]
            )
        return carry

    lax.fori_loop(0, slots // unroll, gather, 0)
    area = area_rows_ref[...]
    wet = jnp.concatenate(
        [
            (rows_ref[pl.ds(block, slots, stride=lane_blocks), :] * area).astype(jnp.bfloat16)
            for block in range(lane_blocks)
        ],
        1,
    )
    total = jnp.dot(pick_ref[...], wet, preferred_element_type=jnp.float32)
    pack(total[:, :cavity], part_ref)


def partial_coupling(modes, shell, count, fluid_nodes, shell_nodes, area):
    cavity, depth = modes.shape
    shells = shell.shape[0]
    slots = fluid_nodes.shape[0]
    rows = rows_needed(shells, cavity, len(offsets_of(PLANE)) + 1)
    lane_blocks = pl.cdiv(cavity, LANES)
    outside = pl.BlockSpec(memory_space=pltpu.HBM)
    inside = pl.BlockSpec(memory_space=pltpu.VMEM)
    return pl.pallas_call(
        gather_kernel,
        in_specs=[outside] * 2 + [pl.BlockSpec(memory_space=pltpu.SMEM)] + [outside] * 3,
        out_specs=[inside] * 2,
        out_shape=[
            jax.ShapeDtypeStruct((rows, LANES), jnp.bfloat16),
            jax.ShapeDtypeStruct(modes.shape, modes.dtype),
        ],
        scratch_shapes=[
            pltpu.VMEM(shell.shape, shell.dtype),
            pltpu.SMEM((slots,), jnp.int32),
            pltpu.VMEM((slots,), jnp.int32),
            pltpu.VMEM((slots,), jnp.float32),
            pltpu.VMEM((depth * lane_blocks, LANES), jnp.float32),
            pltpu.VMEM((slots * lane_blocks, LANES), jnp.float32),
            pltpu.VMEM((shells, slots), jnp.bfloat16),
            pltpu.VMEM((slots, LANES), jnp.float32),
            pltpu.SemaphoreType.DMA((CHUNKS,)),
            pltpu.SemaphoreType.DMA((len((shell, fluid_nodes, shell_nodes, area)),)),
        ],
        compiler_params=pltpu.CompilerParams(vmem_limit_bytes=44 << 20),
    )(outer(modes), outer(shell), count, outer(fluid_nodes), outer(shell_nodes), outer(area))


def solve_kernel(part_ref, *rest):
    terms_hbm = rest[:7]
    amps_ref, structure_ref = rest[7:9]
    terms = rest[9:16]
    plane_ref, mine_ref, stack_ref, full_ref, term_sem, send_sem, recv_sem = rest[16:]

    digits = own_digits()
    plane, stack = offsets_of(PLANE), offsets_of(STACK)
    barrier = pltpu.get_barrier_semaphore()
    for names, offsets in ((PLANE, plane), (STACK, stack)):
        for offset in offsets:
            pl.semaphore_signal(
                barrier,
                inc=1,
                device_id=place_of(moved(digits, names, offset)),
                device_id_type=MESH,
            )
    small = [
        pltpu.make_async_copy(source, target, term_sem.at[at])
        for at, (source, target) in enumerate(zip(terms_hbm, terms))
    ]
    for copy in small:
        copy.start()

    size = mine_ref.shape[0]
    own = rank_of(digits, PLANE)

    def rows_of(rank):
        return pl.ds(pl.multiple_of(rank * size, size), size)

    pl.semaphore_wait(barrier, len(plane) + len(stack))
    for slot, offset in enumerate(plane):
        there = moved(digits, PLANE, offset)
        pltpu.make_async_remote_copy(
            src_ref=part_ref.at[rows_of(rank_of(there, PLANE))],
            dst_ref=plane_ref.at[slot],
            send_sem=send_sem.at[0],
            recv_sem=recv_sem.at[0],
            device_id=place_of(there),
            device_id_type=MESH,
        ).start()

    for copy in small:
        copy.wait()
    shells, cavity = terms[0].shape[0], terms[2].shape[0]
    shell_freq, shell_loss, cavity_freq, cavity_loss, freqs, force, source = [
        term[...].reshape(1, term.shape[0]) for term in terms
    ]
    frequencies = column_of(freqs)
    squared = frequencies * frequencies
    shell_p, shell_q = inverse_terms(shell_freq, shell_loss, squared)
    cavity_p, cavity_q = inverse_terms(cavity_freq, cavity_loss, squared)
    base_re = source * cavity_p
    base_im = -source * cavity_q
    back_p, back_q = squared * cavity_p, squared * cavity_q

    pltpu.make_async_copy(plane_ref, plane_ref, recv_sem.at[0]).wait()
    mine_ref[...] = (
        part_ref[rows_of(own), :].astype(jnp.float32)
        + jnp.sum(plane_ref[...].astype(jnp.float32), axis=0)
    ).astype(jnp.bfloat16)

    for slot, offset in enumerate(stack):
        pltpu.make_async_remote_copy(
            src_ref=mine_ref,
            dst_ref=stack_ref.at[slot],
            send_sem=send_sem.at[1],
            recv_sem=recv_sem.at[1],
            device_id=place_of(moved(digits, STACK, offset)),
            device_id_type=MESH,
        ).start()
    pltpu.make_async_copy(stack_ref, stack_ref, recv_sem.at[1]).wait()
    full_ref[rows_of(own), :] = (
        mine_ref[...].astype(jnp.float32)
        + jnp.sum(stack_ref[...].astype(jnp.float32), axis=0)
    ).astype(jnp.bfloat16)

    for offset in plane:
        pltpu.make_async_remote_copy(
            src_ref=full_ref.at[rows_of(own)],
            dst_ref=full_ref.at[rows_of(own)],
            send_sem=send_sem.at[2],
            recv_sem=recv_sem.at[2],
            device_id=place_of(moved(digits, PLANE, offset)),
            device_id_type=MESH,
        ).start()
    pltpu.make_async_copy(plane_ref, plane_ref, recv_sem.at[2]).wait()

    coupling = unpack(full_ref, shells, cavity)
    total_freqs = squared.shape[0]
    real, imag = base_re, base_im
    for section in range(SECTIONS):
        loads = lax.dot_general(
            jnp.concatenate([real, imag], 0).astype(jnp.bfloat16),
            coupling,
            (((1,), (1,)), ((), ())),
            preferred_element_type=jnp.float32,
        )
        load_re, load_im = force + loads[:total_freqs], loads[total_freqs:]
        struct_re = load_re * shell_p + load_im * shell_q
        struct_im = load_im * shell_p - load_re * shell_q
        back = jnp.dot(
            jnp.concatenate([struct_re, struct_im], 0).astype(jnp.bfloat16),
            coupling,
            preferred_element_type=jnp.float32,
        )
        back_re, back_im = back[:total_freqs], back[total_freqs:]
        coupled_re = back_re * back_p + back_im * back_q
        coupled_im = back_im * back_p - back_re * back_q
        real, imag = base_re + coupled_re, base_im + coupled_im
    for at, values in enumerate((base_re, base_im, coupled_re, coupled_im)):
        amps_ref[pl.ds(at * total_freqs, total_freqs), :] = values.astype(jnp.bfloat16)
    structure_ref[0] = struct_re
    structure_ref[1] = struct_im

    pltpu.make_async_copy(plane_ref, plane_ref, send_sem.at[0]).wait()
    pltpu.make_async_copy(stack_ref, stack_ref, send_sem.at[1]).wait()
    pltpu.make_async_copy(plane_ref, plane_ref, send_sem.at[2]).wait()


def solve(part, terms):
    shells, cavity, total_freqs = terms[0].shape[0], terms[2].shape[0], terms[4].shape[0]
    planes, stacks = len(offsets_of(PLANE)), len(offsets_of(STACK))
    size = part.shape[0] // (planes + 1)
    outside = pl.BlockSpec(memory_space=pltpu.HBM)
    inside = pl.BlockSpec(memory_space=pltpu.VMEM)
    return pl.pallas_call(
        solve_kernel,
        in_specs=[inside] + [outside] * len(terms),
        out_specs=[inside] * 2,
        out_shape=[
            jax.ShapeDtypeStruct((4 * total_freqs, cavity), jnp.bfloat16),
            jax.ShapeDtypeStruct((2, total_freqs, shells), jnp.float32),
        ],
        scratch_shapes=[pltpu.VMEM(term.shape, term.dtype) for term in terms]
        + [
            pltpu.VMEM((planes, size, LANES), jnp.bfloat16),
            pltpu.VMEM((size, LANES), jnp.bfloat16),
            pltpu.VMEM((stacks, size, LANES), jnp.bfloat16),
            pltpu.VMEM(part.shape, jnp.bfloat16),
            pltpu.SemaphoreType.DMA((len(terms),)),
            pltpu.SemaphoreType.DMA((3,)),
            pltpu.SemaphoreType.DMA((3,)),
        ],
        compiler_params=pltpu.CompilerParams(
            collective_id=0, has_side_effects=True, vmem_limit_bytes=24 << 20
        ),
    )(part, *[outer(term) for term in terms])


def field_kernel(amps_ref, modes_ref, structure_ref, pressure_hbm, own_ref, held_ref, out_sem):
    chunk = held_ref.shape[1]
    half = held_ref.shape[2]
    copies = []
    for at in range(held_ref.shape[0]):
        both = jnp.dot(
            amps_ref[...],
            modes_ref[:, at * chunk : (at + 1) * chunk],
            preferred_element_type=jnp.float32,
        )
        held_ref[at] = (both[:half] + both[half:]).T.astype(jnp.bfloat16)
        copies.append(
            pltpu.make_async_copy(
                held_ref.at[at], pressure_hbm.at[pl.ds(at * chunk, chunk)], out_sem.at[at]
            )
        )
        copies[-1].start()
    count = own_ref.shape[1]
    first = pl.multiple_of(lax.axis_index("grp") * count, count)
    own_ref[...] = structure_ref[:, pl.ds(first, count), :]
    for copy in copies:
        copy.wait()


def field(amps, modes, structure, groups):
    depth = modes.shape[1]
    parts, count, shells = structure.shape
    half = amps.shape[0] // 2
    inside = pl.BlockSpec(memory_space=pltpu.VMEM)
    return pl.pallas_call(
        field_kernel,
        in_specs=[inside] * 3,
        out_specs=[pl.BlockSpec(memory_space=pltpu.HBM), inside],
        out_shape=[
            jax.ShapeDtypeStruct((depth, half), jnp.bfloat16),
            jax.ShapeDtypeStruct((parts, count // groups, shells), jnp.float32),
        ],
        scratch_shapes=[
            pltpu.VMEM((CHUNKS, depth // CHUNKS, half), jnp.bfloat16),
            pltpu.SemaphoreType.DMA((CHUNKS,)),
        ],
        compiler_params=pltpu.CompilerParams(vmem_limit_bytes=24 << 20),
    )(amps, modes, structure)


def on_device(acoustic_modes, shell_modes, wet_counts, fluid_nodes, shell_nodes, wet_area, *terms):
    part, modes = partial_coupling(
        acoustic_modes.T, shell_modes.T, wet_counts, fluid_nodes, shell_nodes, wet_area
    )
    amps, structure = solve(part, terms)
    return tuple(field(amps, modes, structure, lax.axis_size("grp")))


def solution(mesh):
    both = P(("fluid", "grp"))
    placed = (P(("fluid", "grp"), None), P("fluid", None)) + (both,) * 4 + (P(),) * 7
    return jax.shard_map(
        on_device,
        mesh=mesh,
        in_specs=placed,
        out_specs=(P(("fluid", "grp"), None), P(None, "grp", None)),
        check_vma=False,
    )
```

time: 94.6 us -> 46.8 us (0.49)
  Pallas kernels: 86.2 us -> 45.4 us
  local copies, waits for them, and re-layouts: 5.84 us -> 0 us
    pallas_call x3, Pallas kernels: 86.2 us -> 45.4 us  [the longest x1 30.7 us: solve(): pl.pallas_call(solve_kernel, in_specs=[inside] + [outside] * len(terms),...]
    unnamed x18 -> x0, local copies, waits for them, and re-layouts: 3.79 us -> none
    broadcast_in_dim x3 -> x0, local copies, waits for them, and re-layouts: 2.05 us -> none  [on_device(): term[None, :]]
where the time goes in v2:
time: 46.8 us; the launch traced here: 46.7 us
  Pallas kernels  45.4 us (97%)
  between operations  1.29 us (3%)
    pallas_call x1, Pallas kernels, solve(): pl.pallas_call(solve_kernel, in_specs=[inside] + [outside] * len(terms),...  30.7 us
    pallas_call x1, Pallas kernels, partial_coupling(): pl.pallas_call(gather_kernel, in_specs=[outside] * 2 + [pl.BlockSpec(memo...  10.8 us
    pallas_call x1, Pallas kernels, field(): pl.pallas_call(field_kernel, in_specs=[inside] * 3, out_specs=[pl.BlockSp...  3.84 us

profile of v2, /device:TPU:1, one launch (start us, length us, event | category | flops | bytes accessed | tf_op | source)
XLA Modules:
  0.0 46.7 jit_solution(16285962591550622760)
XLA Ops:
  1.3 10.8 %shard_map.140 = (bf16[1024,128]{1,0:T(8,128)(2,1)S(1)}, bf16[400,8192]{1,0:T(8,128)(2,1)S(1)}) custom-call(bf16[400,8192]{1,0:T(8,128)(2,1)} %bitcast.2, bf16[300,1024]{1,0:T(8,128)(2,1)} %bitcast.3, s32[1]{0:T(128)S(6)} %copy.15.count_ref, s32[2048]{0:T(1024)} %fluid_hbm.1, s32[2048]{0:T(1024)} %node_hbm.1, f32[2048]{0:T(1024)} %area_hbm.1), custom_call_target="tpu_custom_call" | custom-call | tf_op jit(solution)/shard_map/pallas_call | solution.py:225
  12.1 30.7 %shard_map.141 = (bf16[256,400]{1,0:T(8,128)(2,1)S(1)}, f32[2,64,300]{2,1,0:T(8,128)S(1)}) custom-call(bf16[1024,128]{1,0:T(8,128)(2,1)S(1)} %get-tuple-element.6.part_ref, f32[300]{0:T(512)} %rest_0_.1, f32[300]{0:T(512)} %rest_1_.1, f32[400]{0:T(512)} %rest_2_.1, f32[400]{0:T(512)} %rest_3_.1, f32[64]{0:T(128)} %rest_4_.1, f32[300]{0:T(512)} %rest_5_.1, ...), custom_call_target="tpu_custom_call" | custom-call | tf_op jit(solution)/shard_map/pallas_call | solution.py:375
  42.8 3.8 %shard_map.142 = (bf16[8192,128]{1,0:T(8,128)(2,1)}, f32[2,16,300]{2,1,0:T(8,128)}) custom-call(bf16[256,400]{1,0:T(8,128)(2,1)S(1)} %get-tuple-element.7.amps_ref, bf16[400,8192]{1,0:T(8,128)(2,1)S(1)} %get-tuple-element.8.modes_ref, f32[2,64,300]{2,1,0:T(8,128)S(1)} %get-tuple-element.9.structure_ref), custom_call_target="tpu_custom_call" | custom-call | tf_op jit(solution)/shard_map/pallas_call | solution.py:428

commit v3 on v2

--- a/solution.py
+++ b/solution.py
@@ -19,25 +19,35 @@
     places = [()]
     for name in names:
         places = [place + (step,) for place in places for step in range(SIZES[name])]
-    return places[1:]
+    return sorted(places[1:], key=lambda place: -hops(names, place))
+
+
+def hops(names, place):
+    return sum(
+        min(step, SIZES[name] - step) for name, step in zip(names, place) if name != "c"
+    )
 
 
 def own_digits():
     fluid, grp = lax.axis_index("fluid"), lax.axis_index("grp")
-    return {
+    digits = {
         "z": fluid // 8,
         "xh": (fluid // 4) % 2,
         "y": fluid % 4,
         "xl": grp // 2,
         "c": grp % 2,
     }
+    for name, size in SIZES.items():
+        for step in range(1, size):
+            digits[name, step] = lax.rem(digits[name] + step, size)
+    return digits
 
 
 def moved(digits, names, offset):
     there = dict(digits)
     for name, step in zip(names, offset):
         if step:
-            there[name] = lax.rem(digits[name] + step, SIZES[name])
+            there[name] = digits[name, step]
     return there
 
 
@@ -121,41 +131,40 @@
     return pltpu.with_memory_space_constraint(value, pltpu.HBM)
 
 
-def gather_kernel(
+def main_kernel(
     modes_hbm,
     shell_hbm,
     count_ref,
     fluid_hbm,
     node_hbm,
     area_hbm,
-    part_ref,
-    modes_ref,
-    shell_ref,
-    fluid_ref,
-    node_ref,
-    area_ref,
-    table_ref,
-    rows_ref,
-    pick_ref,
-    area_rows_ref,
-    modes_sem,
-    small_sem,
+    *rest,
 ):
+    terms_hbm = rest[:7]
+    amps_ref, structure_ref, modes_ref = rest[7:10]
+    shell_ref, fluid_ref, node_ref, area_ref = rest[10:14]
+    terms = rest[14:21]
+    table_ref, rows_ref, pick_ref, area_rows_ref = rest[21:25]
+    part_ref, plane_ref, mine_ref, stack_ref, full_ref = rest[25:30]
+    modes_sem, small_sem, send_sem, recv_sem = rest[30:]
+
     cavity, depth = modes_ref.shape
     shells, shell_depth = shell_ref.shape
     slots = fluid_ref.shape[0]
     chunk, span = depth // CHUNKS, slots // CHUNKS
     lane_blocks = pl.cdiv(cavity, LANES)
 
-    pairs = [
-        (shell_hbm, shell_ref),
-        (node_hbm, node_ref),
-        (area_hbm, area_ref),
-        (fluid_hbm, fluid_ref),
-    ]
     small = [
         pltpu.make_async_copy(source, target, small_sem.at[at])
-        for at, (source, target) in enumerate(pairs)
+        for at, (source, target) in enumerate(
+            [
+                (shell_hbm, shell_ref),
+                (node_hbm, node_ref),
+                (area_hbm, area_ref),
+                (fluid_hbm, fluid_ref),
+            ]
+            + list(zip(terms_hbm, terms))
+        )
     ]
     large = [
         pltpu.make_async_copy(
@@ -165,8 +174,23 @@
         )
         for at in range(CHUNKS)
     ]
-    for copy in small + large:
+    small[0].start()
+    large[0].start()
+    for copy in small[1:] + large[1:]:
         copy.start()
+
+    digits = own_digits()
+    plane, stack = offsets_of(PLANE), offsets_of(STACK)
+    barrier = pltpu.get_barrier_semaphore()
+    for names, offsets in ((PLANE, plane), (STACK, stack)):
+        for offset in offsets:
+            pl.semaphore_signal(
+                barrier,
+                inc=1,
+                device_id=place_of(moved(digits, names, offset)),
+                device_id_type=MESH,
+            )
+
     for copy in small:
         copy.wait()
     count = count_ref[0]
@@ -191,13 +215,17 @@
             )
 
     unroll = 16
+    pairs_ref = table_ref.reshape(depth // 2, 2 * lane_blocks, LANES)
 
     def gather(step, carry):
         for at in range(unroll):
             slot = step * unroll + at
-            first = pl.multiple_of(fluid_ref[slot] * lane_blocks, lane_blocks)
+            node = fluid_ref[slot]
+            pair = pairs_ref[lax.shift_right_logical(node, 1)]
             rows_ref[pl.ds(pl.multiple_of(slot * lane_blocks, lane_blocks), lane_blocks), :] = (
-                table_ref[pl.ds(first, lane_blocks), :]
+                jnp.where(
+                    jnp.bitwise_and(node, 1) == 1, pair[lane_blocks:], pair[:lane_blocks]
+                )
             )
         return carry
 
@@ -213,63 +241,6 @@
     total = jnp.dot(pick_ref[...], wet, preferred_element_type=jnp.float32)
     pack(total[:, :cavity], part_ref)
 
-
-def partial_coupling(modes, shell, count, fluid_nodes, shell_nodes, area):
-    cavity, depth = modes.shape
-    shells = shell.shape[0]
-    slots = fluid_nodes.shape[0]
-    rows = rows_needed(shells, cavity, len(offsets_of(PLANE)) + 1)
-    lane_blocks = pl.cdiv(cavity, LANES)
-    outside = pl.BlockSpec(memory_space=pltpu.HBM)
-    inside = pl.BlockSpec(memory_space=pltpu.VMEM)
-    return pl.pallas_call(
-        gather_kernel,
-        in_specs=[outside] * 2 + [pl.BlockSpec(memory_space=pltpu.SMEM)] + [outside] * 3,
-        out_specs=[inside] * 2,
-        out_shape=[
-            jax.ShapeDtypeStruct((rows, LANES), jnp.bfloat16),
-            jax.ShapeDtypeStruct(modes.shape, modes.dtype),
-        ],
-        scratch_shapes=[
-            pltpu.VMEM(shell.shape, shell.dtype),
-            pltpu.SMEM((slots,), jnp.int32),
-            pltpu.VMEM((slots,), jnp.int32),
-            pltpu.VMEM((slots,), jnp.float32),
-            pltpu.VMEM((depth * lane_blocks, LANES), jnp.float32),
-            pltpu.VMEM((slots * lane_blocks, LANES), jnp.float32),
-            pltpu.VMEM((shells, slots), jnp.bfloat16),
-            pltpu.VMEM((slots, LANES), jnp.float32),
-            pltpu.SemaphoreType.DMA((CHUNKS,)),
-            pltpu.SemaphoreType.DMA((len((shell, fluid_nodes, shell_nodes, area)),)),
-        ],
-        compiler_params=pltpu.CompilerParams(vmem_limit_bytes=44 << 20),
-    )(outer(modes), outer(shell), count, outer(fluid_nodes), outer(shell_nodes), outer(area))
-
-
-def solve_kernel(part_ref, *rest):
-    terms_hbm = rest[:7]
-    amps_ref, structure_ref = rest[7:9]
-    terms = rest[9:16]
-    plane_ref, mine_ref, stack_ref, full_ref, term_sem, send_sem, recv_sem = rest[16:]
-
-    digits = own_digits()
-    plane, stack = offsets_of(PLANE), offsets_of(STACK)
-    barrier = pltpu.get_barrier_semaphore()
-    for names, offsets in ((PLANE, plane), (STACK, stack)):
-        for offset in offsets:
-            pl.semaphore_signal(
-                barrier,
-                inc=1,
-                device_id=place_of(moved(digits, names, offset)),
-                device_id_type=MESH,
-            )
-    small = [
-        pltpu.make_async_copy(source, target, term_sem.at[at])
-        for at, (source, target) in enumerate(zip(terms_hbm, terms))
-    ]
-    for copy in small:
-        copy.start()
-
     size = mine_ref.shape[0]
     own = rank_of(digits, PLANE)
 
@@ -288,9 +259,6 @@
             device_id_type=MESH,
         ).start()
 
-    for copy in small:
-        copy.wait()
-    shells, cavity = terms[0].shape[0], terms[2].shape[0]
     shell_freq, shell_loss, cavity_freq, cavity_loss, freqs, force, source = [
         term[...].reshape(1, term.shape[0]) for term in terms
     ]
@@ -366,34 +334,58 @@
     pltpu.make_async_copy(plane_ref, plane_ref, send_sem.at[2]).wait()
 
 
-def solve(part, terms):
-    shells, cavity, total_freqs = terms[0].shape[0], terms[2].shape[0], terms[4].shape[0]
+def amplitudes(modes, shell, count, fluid_nodes, shell_nodes, area, terms, total_freqs):
+    cavity, depth = modes.shape
+    shells = shell.shape[0]
+    slots = fluid_nodes.shape[0]
     planes, stacks = len(offsets_of(PLANE)), len(offsets_of(STACK))
-    size = part.shape[0] // (planes + 1)
+    rows = rows_needed(shells, cavity, planes + 1)
+    size = rows // (planes + 1)
+    lane_blocks = pl.cdiv(cavity, LANES)
     outside = pl.BlockSpec(memory_space=pltpu.HBM)
     inside = pl.BlockSpec(memory_space=pltpu.VMEM)
     return pl.pallas_call(
-        solve_kernel,
-        in_specs=[inside] + [outside] * len(terms),
-        out_specs=[inside] * 2,
+        main_kernel,
+        in_specs=[outside] * 2
+        + [pl.BlockSpec(memory_space=pltpu.SMEM)]
+        + [outside] * (3 + len(terms)),
+        out_specs=[inside] * 3,
         out_shape=[
             jax.ShapeDtypeStruct((4 * total_freqs, cavity), jnp.bfloat16),
             jax.ShapeDtypeStruct((2, total_freqs, shells), jnp.float32),
+            jax.ShapeDtypeStruct(modes.shape, modes.dtype),
         ],
-        scratch_shapes=[pltpu.VMEM(term.shape, term.dtype) for term in terms]
+        scratch_shapes=[
+            pltpu.VMEM(shell.shape, shell.dtype),
+            pltpu.SMEM((slots,), jnp.int32),
+            pltpu.VMEM((slots,), jnp.int32),
+            pltpu.VMEM((slots,), jnp.float32),
+        ]
+        + [pltpu.VMEM(term.shape, term.dtype) for term in terms]
         + [
+            pltpu.VMEM((depth * lane_blocks, LANES), jnp.float32),
+            pltpu.VMEM((slots * lane_blocks, LANES), jnp.float32),
+            pltpu.VMEM((shells, slots), jnp.bfloat16),
+            pltpu.VMEM((slots, LANES), jnp.float32),
+            pltpu.VMEM((rows, LANES), jnp.bfloat16),
             pltpu.VMEM((planes, size, LANES), jnp.bfloat16),
             pltpu.VMEM((size, LANES), jnp.bfloat16),
             pltpu.VMEM((stacks, size, LANES), jnp.bfloat16),
-            pltpu.VMEM(part.shape, jnp.bfloat16),
-            pltpu.SemaphoreType.DMA((len(terms),)),
+            pltpu.VMEM((rows, LANES), jnp.bfloat16),
+            pltpu.SemaphoreType.DMA((CHUNKS,)),
+            pltpu.SemaphoreType.DMA((4 + len(terms),)),
             pltpu.SemaphoreType.DMA((3,)),
             pltpu.SemaphoreType.DMA((3,)),
         ],
         compiler_params=pltpu.CompilerParams(
-            collective_id=0, has_side_effects=True, vmem_limit_bytes=24 << 20
+            collective_id=0, has_side_effects=True, vmem_limit_bytes=44 << 20
         ),
-    )(part, *[outer(term) for term in terms])
+    )(
+        outer(modes),
+        outer(shell),
+        count,
+        *[outer(value) for value in (fluid_nodes, shell_nodes, area, *terms)],
+    )
 
 
 def field_kernel(amps_ref, modes_ref, structure_ref, pressure_hbm, own_ref, held_ref, out_sem):
@@ -442,10 +434,16 @@
 
 
 def on_device(acoustic_modes, shell_modes, wet_counts, fluid_nodes, shell_nodes, wet_area, *terms):
-    part, modes = partial_coupling(
-        acoustic_modes.T, shell_modes.T, wet_counts, fluid_nodes, shell_nodes, wet_area
+    amps, structure, modes = amplitudes(
+        acoustic_modes.T,
+        shell_modes.T,
+        wet_counts,
+        fluid_nodes,
+        shell_nodes,
+        wet_area,
+        terms,
+        terms[4].shape[0],
     )
-    amps, structure = solve(part, terms)
     return tuple(field(amps, modes, structure, lax.axis_size("grp")))
 
 

time: 46.8 us -> 41.9 us (0.90)
  Pallas kernels: 45.4 us -> 40.5 us
    pallas_call x2 -> x1, Pallas kernels: 41.5 us -> 36.7 us  [amplitudes(): pl.pallas_call(main_kernel, in_specs=[outside] * 2 + [pl.BlockSpec(memory...]
where the time goes in v3:
time: 41.9 us; the launch traced here: 41.8 us
  Pallas kernels  40.5 us (97%)
  between operations  1.29 us (3%)
    pallas_call x1, Pallas kernels, amplitudes(): pl.pallas_call(main_kernel, in_specs=[outside] * 2 + [pl.BlockSpec(memory...  36.7 us
    pallas_call x1, Pallas kernels, field(): pl.pallas_call(field_kernel, in_specs=[inside] * 3, out_specs=[pl.BlockSp...  3.83 us

profile of v3, /device:TPU:1, one launch (start us, length us, event | category | flops | bytes accessed | tf_op | source)
XLA Modules:
  0.0 41.8 jit_solution(6843825270258300645)
XLA Ops:
  1.3 36.7 %shard_map.140 = (bf16[256,400]{1,0:T(8,128)(2,1)S(1)}, f32[2,64,300]{2,1,0:T(8,128)S(1)}, bf16[400,8192]{1,0:T(8,128)(2,1)S(1)}) custom-call(bf16[400,8192]{1,0:T(8,128)(2,1)} %bitcast.2, bf16[300,1024]{1,0:T(8,128)(2,1)} %bitcast.3, s32[1]{0:T(128)S(6)} %copy.15.count_ref, s32[2048]{0:T(1024)} %fluid_hbm.1, s32[2048]{0:T(1024)} %node_hbm.1, ...), custom_call_target="tpu_custom_call" | custom-call | tf_op jit(solution)/shard_map/pallas_call | solution.py:347
  38.0 3.8 %shard_map.141 = (bf16[8192,128]{1,0:T(8,128)(2,1)}, f32[2,16,300]{2,1,0:T(8,128)}) custom-call(bf16[256,400]{1,0:T(8,128)(2,1)S(1)} %get-tuple-element.5.amps_ref, bf16[400,8192]{1,0:T(8,128)(2,1)S(1)} %get-tuple-element.6.modes_ref, f32[2,64,300]{2,1,0:T(8,128)S(1)} %get-tuple-element.7.structure_ref), custom_call_target="tpu_custom_call" | custom-call | tf_op jit(solution)/shard_map/pallas_call | solution.py:420

commit v4 on v3

--- a/solution.py
+++ b/solution.py
@@ -11,7 +11,8 @@
 SIZES = {"z": 8, "xh": 2, "y": 4, "xl": 2, "c": 2}
 PLANE = ("xh", "y", "xl", "c")
 STACK = ("z",)
-CHUNKS = 8
+CHUNKS = 4
+PARTS = 8
 TAIL = 4
 
 
@@ -141,17 +142,17 @@
     *rest,
 ):
     terms_hbm = rest[:7]
-    amps_ref, structure_ref, modes_ref = rest[7:10]
-    shell_ref, fluid_ref, node_ref, area_ref = rest[10:14]
-    terms = rest[14:21]
-    table_ref, rows_ref, pick_ref, area_rows_ref = rest[21:25]
-    part_ref, plane_ref, mine_ref, stack_ref, full_ref = rest[25:30]
-    modes_sem, small_sem, send_sem, recv_sem = rest[30:]
+    amps_ref, structure_ref, modes_ref, free_ref = rest[7:11]
+    shell_ref, fluid_ref, node_ref, area_ref = rest[11:15]
+    terms = rest[15:22]
+    table_ref, rows_ref, pick_ref, area_rows_ref = rest[22:26]
+    part_ref, plane_ref, mine_ref, stack_ref, full_ref = rest[26:31]
+    modes_sem, small_sem, send_sem, recv_sem = rest[31:]
 
     cavity, depth = modes_ref.shape
     shells, shell_depth = shell_ref.shape
     slots = fluid_ref.shape[0]
-    chunk, span = depth // CHUNKS, slots // CHUNKS
+    chunk, span = depth // CHUNKS, slots // PARTS
     lane_blocks = pl.cdiv(cavity, LANES)
 
     small = [
@@ -174,9 +175,7 @@
         )
         for at in range(CHUNKS)
     ]
-    small[0].start()
-    large[0].start()
-    for copy in small[1:] + large[1:]:
+    for copy in large[:1] + small + large[1:]:
         copy.start()
 
     digits = own_digits()
@@ -191,20 +190,7 @@
                 device_id_type=MESH,
             )
 
-    for copy in small:
-        copy.wait()
-    count = count_ref[0]
     for at in range(CHUNKS):
-        here = pl.ds(at * span, span)
-        slot = lax.broadcasted_iota(jnp.int32, (1, span), 1) + at * span
-        node = jnp.where(slot < count, node_ref[here].reshape(1, span), -1)
-        number = lax.broadcasted_iota(jnp.int32, (shell_depth, span), 0)
-        hot = jnp.where(number == node, 1.0, 0.0).astype(jnp.bfloat16)
-        pick_ref[:, here] = jnp.dot(
-            shell_ref[...], hot, preferred_element_type=jnp.float32
-        ).astype(jnp.bfloat16)
-        area = area_ref[here].reshape(1, span)
-        area_rows_ref[here, :] = jnp.broadcast_to(area, (LANES, span)).T
         large[at].wait()
         for block in range(lane_blocks):
             first = block * LANES
@@ -213,23 +199,32 @@
             table_ref[pl.ds(at * chunk * lane_blocks + block, chunk, stride=lane_blocks), :] = (
                 pad_lanes(piece.astype(jnp.float32), LANES)
             )
-
-    unroll = 16
-    pairs_ref = table_ref.reshape(depth // 2, 2 * lane_blocks, LANES)
+    for copy in small:
+        copy.wait()
+    count = count_ref[0]
+    for at in range(PARTS):
+        here = pl.ds(at * span, span)
+        area_rows_ref[here, :] = jnp.broadcast_to(
+            area_ref[here].reshape(1, span), (LANES, span)
+        ).T
 
     def gather(step, carry):
-        for at in range(unroll):
-            slot = step * unroll + at
-            node = fluid_ref[slot]
-            pair = pairs_ref[lax.shift_right_logical(node, 1)]
-            rows_ref[pl.ds(pl.multiple_of(slot * lane_blocks, lane_blocks), lane_blocks), :] = (
-                jnp.where(
-                    jnp.bitwise_and(node, 1) == 1, pair[lane_blocks:], pair[:lane_blocks]
-                )
+        here = pl.ds(pl.multiple_of(step * span, span), span)
+        slot = lax.broadcasted_iota(jnp.int32, (1, span), 1) + step * span
+        node = jnp.where(slot < count, node_ref[here].reshape(1, span), -1)
+        number = lax.broadcasted_iota(jnp.int32, (shell_depth, span), 0)
+        hot = jnp.where(number == node, 1.0, 0.0).astype(jnp.bfloat16)
+        pick_ref[:, here] = jnp.dot(
+            shell_ref[...], hot, preferred_element_type=jnp.float32
+        ).astype(jnp.bfloat16)
+        for at in range(span):
+            row = step * span + at
+            rows_ref[pl.ds(pl.multiple_of(row * lane_blocks, lane_blocks), lane_blocks), :] = (
+                table_ref[pl.ds(fluid_ref[row] * lane_blocks, lane_blocks), :]
             )
         return carry
 
-    lax.fori_loop(0, slots // unroll, gather, 0)
+    lax.fori_loop(0, PARTS, gather, 0)
     area = area_rows_ref[...]
     wet = jnp.concatenate(
         [
@@ -285,6 +280,12 @@
             device_id=place_of(moved(digits, STACK, offset)),
             device_id_type=MESH,
         ).start()
+
+    free = jnp.concatenate([base_re, base_im], 0).astype(jnp.bfloat16)
+    for at in range(PARTS):
+        here = pl.ds(at * (depth // PARTS), depth // PARTS)
+        free_ref[:, here] = jnp.dot(free, modes_ref[:, here], preferred_element_type=jnp.float32)
+
     pltpu.make_async_copy(stack_ref, stack_ref, recv_sem.at[1]).wait()
     full_ref[rows_of(own), :] = (
         mine_ref[...].astype(jnp.float32)
@@ -324,8 +325,8 @@
         coupled_re = back_re * back_p + back_im * back_q
         coupled_im = back_im * back_p - back_re * back_q
         real, imag = base_re + coupled_re, base_im + coupled_im
-    for at, values in enumerate((base_re, base_im, coupled_re, coupled_im)):
-        amps_ref[pl.ds(at * total_freqs, total_freqs), :] = values.astype(jnp.bfloat16)
+    amps_ref[pl.ds(0, total_freqs), :] = coupled_re.astype(jnp.bfloat16)
+    amps_ref[pl.ds(total_freqs, total_freqs), :] = coupled_im.astype(jnp.bfloat16)
     structure_ref[0] = struct_re
     structure_ref[1] = struct_im
 
@@ -349,11 +350,12 @@
         in_specs=[outside] * 2
         + [pl.BlockSpec(memory_space=pltpu.SMEM)]
         + [outside] * (3 + len(terms)),
-        out_specs=[inside] * 3,
+        out_specs=[inside] * 4,
         out_shape=[
-            jax.ShapeDtypeStruct((4 * total_freqs, cavity), jnp.bfloat16),
+            jax.ShapeDtypeStruct((2 * total_freqs, cavity), jnp.bfloat16),
             jax.ShapeDtypeStruct((2, total_freqs, shells), jnp.float32),
             jax.ShapeDtypeStruct(modes.shape, modes.dtype),
+            jax.ShapeDtypeStruct((2 * total_freqs, depth), jnp.float32),
         ],
         scratch_shapes=[
             pltpu.VMEM(shell.shape, shell.dtype),
@@ -388,21 +390,19 @@
     )
 
 
-def field_kernel(amps_ref, modes_ref, structure_ref, pressure_hbm, own_ref, held_ref, out_sem):
+def field_kernel(
+    amps_ref, modes_ref, free_ref, structure_ref, pressure_hbm, own_ref, held_ref, out_sem
+):
     chunk = held_ref.shape[1]
-    half = held_ref.shape[2]
     copies = []
     for at in range(held_ref.shape[0]):
-        both = jnp.dot(
-            amps_ref[...],
-            modes_ref[:, at * chunk : (at + 1) * chunk],
-            preferred_element_type=jnp.float32,
-        )
-        held_ref[at] = (both[:half] + both[half:]).T.astype(jnp.bfloat16)
+        here = pl.ds(at * chunk, chunk)
+        coupled = jnp.dot(
+            amps_ref[...], modes_ref[:, here], preferred_element_type=jnp.float32
+        )
+        held_ref[at] = (free_ref[:, here] + coupled).T.astype(jnp.bfloat16)
         copies.append(
-            pltpu.make_async_copy(
-                held_ref.at[at], pressure_hbm.at[pl.ds(at * chunk, chunk)], out_sem.at[at]
-            )
+            pltpu.make_async_copy(held_ref.at[at], pressure_hbm.at[here], out_sem.at[at])
         )
         copies[-1].start()
     count = own_ref.shape[1]
@@ -412,29 +412,29 @@
         copy.wait()
 
 
-def field(amps, modes, structure, groups):
+def field(amps, modes, free, structure, groups):
     depth = modes.shape[1]
     parts, count, shells = structure.shape
-    half = amps.shape[0] // 2
+    half = amps.shape[0]
     inside = pl.BlockSpec(memory_space=pltpu.VMEM)
     return pl.pallas_call(
         field_kernel,
-        in_specs=[inside] * 3,
+        in_specs=[inside] * 4,
         out_specs=[pl.BlockSpec(memory_space=pltpu.HBM), inside],
         out_shape=[
             jax.ShapeDtypeStruct((depth, half), jnp.bfloat16),
             jax.ShapeDtypeStruct((parts, count // groups, shells), jnp.float32),
         ],
         scratch_shapes=[
-            pltpu.VMEM((CHUNKS, depth // CHUNKS, half), jnp.bfloat16),
-            pltpu.SemaphoreType.DMA((CHUNKS,)),
+            pltpu.VMEM((PARTS, depth // PARTS, half), jnp.bfloat16),
+            pltpu.SemaphoreType.DMA((PARTS,)),
         ],
         compiler_params=pltpu.CompilerParams(vmem_limit_bytes=24 << 20),
-    )(amps, modes, structure)
+    )(amps, modes, free, structure)
 
 
 def on_device(acoustic_modes, shell_modes, wet_counts, fluid_nodes, shell_nodes, wet_area, *terms):
-    amps, structure, modes = amplitudes(
+    amps, structure, modes, free = amplitudes(
         acoustic_modes.T,
         shell_modes.T,
         wet_counts,
@@ -444,7 +444,7 @@
         terms,
         terms[4].shape[0],
     )
-    return tuple(field(amps, modes, structure, lax.axis_size("grp")))
+    return tuple(field(amps, modes, free, structure, lax.axis_size("grp")))
 
 
 def solution(mesh):

time: 41.9 us -> 43 us (1.026)
  local copies, waits for them, and re-layouts: 0 us -> 2.85 us
  Pallas kernels: 40.5 us -> 38.7 us
    unnamed x0 -> x2, local copies, waits for them, and re-layouts: none -> 2.85 us
    pallas_call x1, Pallas kernels: 3.83 us -> 2.77 us  [field(): pl.pallas_call(field_kernel, in_specs=[inside] * 4, out_specs=[pl.BlockSp...]
    pallas_call x1, Pallas kernels: 36.7 us -> 35.9 us  [amplitudes(): pl.pallas_call(main_kernel, in_specs=[outside] * 2 + [pl.BlockSpec(memory...]
where the time goes in v4:
time: 43 us; the launch traced here: 42.9 us
  Pallas kernels  38.7 us (90%)
  local copies, waits for them, and re-layouts  2.85 us (7%)
  between operations  1.3 us (3%)
    pallas_call x1, Pallas kernels, amplitudes(): pl.pallas_call(main_kernel, in_specs=[outside] * 2 + [pl.BlockSpec(memory...  35.9 us
    unnamed x2, local copies, waits for them, and re-layouts  2.85 us
    pallas_call x1, Pallas kernels, field(): pl.pallas_call(field_kernel, in_specs=[inside] * 4, out_specs=[pl.BlockSp...  2.77 us

profile of v4, /device:TPU:1, one launch (start us, length us, event | category | flops | bytes accessed | tf_op | source)
XLA Modules:
  0.0 42.9 jit_solution(11975155987886926783)
XLA Ops:
  1.3 35.9 %shard_map.140 = (bf16[128,400]{1,0:T(8,128)(2,1)S(1)}, f32[2,64,300]{2,1,0:T(8,128)S(1)}, bf16[400,8192]{1,0:T(8,128)(2,1)}, f32[128,8192]{1,0:T(8,128)S(1)}) custom-call(bf16[400,8192]{1,0:T(8,128)(2,1)} %bitcast.2, bf16[300,1024]{1,0:T(8,128)(2,1)} %bitcast.3, s32[1]{0:T(128)S(6)} %copy.15.count_ref, s32[2048]{0:T(1024)} %fluid_hbm.1, s32[2048]{0:T(1024)} %node_hbm.1, ...), custom_call_target="tpu_custom_call" | custom-call | tf_op jit(solution)/shard_map/pallas_call | solution.py:348
  37.2 0.0 copy-start
  37.2 2.9 %copy-done = bf16[400,8192]{1,0:T(8,128)(2,1)S(1)} copy-done((bf16[400,8192]{1,0:T(8,128)(2,1)S(1)}, bf16[400,8192]{1,0:T(8,128)(2,1)}, u32[]{:S(2)}) %copy-start) | copy-done | bytes 6553624
  40.1 2.8 %shard_map.141 = (bf16[8192,128]{1,0:T(8,128)(2,1)}, f32[2,16,300]{2,1,0:T(8,128)}) custom-call(bf16[128,400]{1,0:T(8,128)(2,1)S(1)} %get-tuple-element.6.amps_ref, bf16[400,8192]{1,0:T(8,128)(2,1)S(1)} %copy-done, f32[128,8192]{1,0:T(8,128)S(1)} %get-tuple-element.8.free_ref, f32[2,64,300]{2,1,0:T(8,128)S(1)} %get-tuple-element.9.structure_ref), custom_call_target="tpu_custom_call" | custom-call | tf_op jit(solution)/shard_map/pallas_call | solution.py:420
Async XLA Ops:
  37.2 2.9 %copy-start = (bf16[400,8192]{1,0:T(8,128)(2,1)S(1)}, bf16[400,8192]{1,0:T(8,128)(2,1)}, u32[]{:S(2)}) copy-start(bf16[400,8192]{1,0:T(8,128)(2,1)} %get-tuple-element.7.modes_ref) | copy-start | bytes 19660804

commit v5 on v4

--- a/solution.py
+++ b/solution.py
@@ -380,7 +380,7 @@
             pltpu.SemaphoreType.DMA((3,)),
         ],
         compiler_params=pltpu.CompilerParams(
-            collective_id=0, has_side_effects=True, vmem_limit_bytes=44 << 20
+            collective_id=0, has_side_effects=True, vmem_limit_bytes=34 << 20
         ),
     )(
         outer(modes),
@@ -429,7 +429,7 @@
             pltpu.VMEM((PARTS, depth // PARTS, half), jnp.bfloat16),
             pltpu.SemaphoreType.DMA((PARTS,)),
         ],
-        compiler_params=pltpu.CompilerParams(vmem_limit_bytes=24 << 20),
+        compiler_params=pltpu.CompilerParams(vmem_limit_bytes=16 << 20),
     )(amps, modes, free, structure)
 
 

time: 43 us -> 37.2 us (0.87)
  Pallas kernels: 38.7 us -> 35.8 us
  local copies, waits for them, and re-layouts: 2.85 us -> 0 us
    pallas_call x1, Pallas kernels: 35.9 us -> 33 us  [amplitudes(): pl.pallas_call(main_kernel, in_specs=[outside] * 2 + [pl.BlockSpec(memory...]
    unnamed x2 -> x0, local copies, waits for them, and re-layouts: 2.85 us -> none
where the time goes in v5:
time: 37.2 us; the launch traced here: 37.1 us
  Pallas kernels  35.8 us (96%)
  between operations  1.29 us (3%)
    pallas_call x1, Pallas kernels, amplitudes(): pl.pallas_call(main_kernel, in_specs=[outside] * 2 + [pl.BlockSpec(memory...  33 us
    pallas_call x1, Pallas kernels, field(): pl.pallas_call(field_kernel, in_specs=[inside] * 4, out_specs=[pl.BlockSp...  2.77 us

profile of v5, /device:TPU:1, one launch (start us, length us, event | category | flops | bytes accessed | tf_op | source)
XLA Modules:
  0.0 37.1 jit_solution(15247467118236339241)
XLA Ops:
  1.3 33.0 %shard_map.140 = (bf16[128,400]{1,0:T(8,128)(2,1)S(1)}, f32[2,64,300]{2,1,0:T(8,128)S(1)}, bf16[400,8192]{1,0:T(8,128)(2,1)S(1)}, f32[128,8192]{1,0:T(8,128)S(1)}) custom-call(bf16[400,8192]{1,0:T(8,128)(2,1)} %bitcast.2, bf16[300,1024]{1,0:T(8,128)(2,1)} %bitcast.3, s32[1]{0:T(128)S(6)} %copy.15.count_ref, s32[2048]{0:T(1024)} %fluid_hbm.1, s32[2048]{0:T(1024)} %node_hbm.1, ...), custom_call_target="tpu_custom_call" | custom-call | tf_op jit(solution)/shard_map/pallas_call | solution.py:348
  34.3 2.8 %shard_map.141 = (bf16[8192,128]{1,0:T(8,128)(2,1)}, f32[2,16,300]{2,1,0:T(8,128)}) custom-call(bf16[128,400]{1,0:T(8,128)(2,1)S(1)} %get-tuple-element.6.amps_ref, bf16[400,8192]{1,0:T(8,128)(2,1)S(1)} %get-tuple-element.7.modes_ref, f32[128,8192]{1,0:T(8,128)S(1)} %get-tuple-element.8.free_ref, f32[2,64,300]{2,1,0:T(8,128)S(1)} %get-tuple-element.9.structure_ref), custom_call_target="tpu_custom_call" | custom-call | tf_op jit(solution)/shard_map/pallas_call | solution.py:420

commit v6 on v5

--- a/solution.py
+++ b/solution.py
@@ -13,6 +13,7 @@
 STACK = ("z",)
 CHUNKS = 4
 PARTS = 8
+STEPS = 4
 TAIL = 4
 
 
@@ -152,7 +153,7 @@
     cavity, depth = modes_ref.shape
     shells, shell_depth = shell_ref.shape
     slots = fluid_ref.shape[0]
-    chunk, span = depth // CHUNKS, slots // PARTS
+    chunk, span = depth // CHUNKS, slots // STEPS
     lane_blocks = pl.cdiv(cavity, LANES)
 
     small = [
@@ -202,11 +203,6 @@
     for copy in small:
         copy.wait()
     count = count_ref[0]
-    for at in range(PARTS):
-        here = pl.ds(at * span, span)
-        area_rows_ref[here, :] = jnp.broadcast_to(
-            area_ref[here].reshape(1, span), (LANES, span)
-        ).T
 
     def gather(step, carry):
         here = pl.ds(pl.multiple_of(step * span, span), span)
@@ -217,6 +213,8 @@
         pick_ref[:, here] = jnp.dot(
             shell_ref[...], hot, preferred_element_type=jnp.float32
         ).astype(jnp.bfloat16)
+        area = area_ref[here].reshape(1, span)
+        area_rows_ref[here, :] = jnp.broadcast_to(area, (LANES, span)).T
         for at in range(span):
             row = step * span + at
             rows_ref[pl.ds(pl.multiple_of(row * lane_blocks, lane_blocks), lane_blocks), :] = (
@@ -224,7 +222,7 @@
             )
         return carry
 
-    lax.fori_loop(0, PARTS, gather, 0)
+    lax.fori_loop(0, STEPS, gather, 0)
     area = area_rows_ref[...]
     wet = jnp.concatenate(
         [
@@ -391,10 +389,17 @@
 
 
 def field_kernel(
-    amps_ref, modes_ref, free_ref, structure_ref, pressure_hbm, own_ref, held_ref, out_sem
+    amps_ref, modes_ref, free_ref, structure_ref, pressure_hbm, own_hbm, held_ref, out_sem
 ):
     chunk = held_ref.shape[1]
-    copies = []
+    count = own_hbm.shape[1]
+    first = pl.multiple_of(lax.axis_index("grp") * count, count)
+    copies = [
+        pltpu.make_async_copy(
+            structure_ref.at[:, pl.ds(first, count), :], own_hbm, out_sem.at[held_ref.shape[0]]
+        )
+    ]
+    copies[0].start()
     for at in range(held_ref.shape[0]):
         here = pl.ds(at * chunk, chunk)
         coupled = jnp.dot(
@@ -405,9 +410,6 @@
             pltpu.make_async_copy(held_ref.at[at], pressure_hbm.at[here], out_sem.at[at])
         )
         copies[-1].start()
-    count = own_ref.shape[1]
-    first = pl.multiple_of(lax.axis_index("grp") * count, count)
-    own_ref[...] = structure_ref[:, pl.ds(first, count), :]
     for copy in copies:
         copy.wait()
 
@@ -420,14 +422,14 @@
     return pl.pallas_call(
         field_kernel,
         in_specs=[inside] * 4,
-        out_specs=[pl.BlockSpec(memory_space=pltpu.HBM), inside],
+        out_specs=[pl.BlockSpec(memory_space=pltpu.HBM)] * 2,
         out_shape=[
             jax.ShapeDtypeStruct((depth, half), jnp.bfloat16),
             jax.ShapeDtypeStruct((parts, count // groups, shells), jnp.float32),
         ],
         scratch_shapes=[
             pltpu.VMEM((PARTS, depth // PARTS, half), jnp.bfloat16),
-            pltpu.SemaphoreType.DMA((PARTS,)),
+            pltpu.SemaphoreType.DMA((PARTS + 1,)),
         ],
         compiler_params=pltpu.CompilerParams(vmem_limit_bytes=16 << 20),
     )(amps, modes, free, structure)

time: 37.2 us -> 36.3 us (0.976)
  Pallas kernels: 35.8 us -> 34.9 us
    pallas_call x1, Pallas kernels: 2.77 us -> 2.16 us  [field(): pl.pallas_call(field_kernel, in_specs=[inside] * 4, out_specs=[pl.BlockSp...]
where the time goes in v6:
time: 36.3 us; the launch traced here: 36.2 us
  Pallas kernels  34.9 us (96%)
  between operations  1.29 us (4%)
    pallas_call x1, Pallas kernels, amplitudes(): pl.pallas_call(main_kernel, in_specs=[outside] * 2 + [pl.BlockSpec(memory...  32.7 us
    pallas_call x1, Pallas kernels, field(): pl.pallas_call(field_kernel, in_specs=[inside] * 4, out_specs=[pl.BlockSp...  2.16 us

profile of v6, /device:TPU:1, one launch (start us, length us, event | category | flops | bytes accessed | tf_op | source)
XLA Modules:
  0.0 36.2 jit_solution(15251882360997589779)
XLA Ops:
  1.3 32.7 %shard_map.140 = (bf16[128,400]{1,0:T(8,128)(2,1)S(1)}, f32[2,64,300]{2,1,0:T(8,128)S(1)}, bf16[400,8192]{1,0:T(8,128)(2,1)S(1)}, f32[128,8192]{1,0:T(8,128)S(1)}) custom-call(bf16[400,8192]{1,0:T(8,128)(2,1)} %bitcast.2, bf16[300,1024]{1,0:T(8,128)(2,1)} %bitcast.3, s32[1]{0:T(128)S(6)} %copy.15.count_ref, s32[2048]{0:T(1024)} %fluid_hbm.1, s32[2048]{0:T(1024)} %node_hbm.1, ...), custom_call_target="tpu_custom_call" | custom-call | tf_op jit(solution)/shard_map/pallas_call | solution.py:346
  34.0 2.2 %shard_map.141 = (bf16[8192,128]{1,0:T(8,128)(2,1)}, f32[2,16,300]{2,1,0:T(8,128)}) custom-call(bf16[128,400]{1,0:T(8,128)(2,1)S(1)} %get-tuple-element.6.amps_ref, bf16[400,8192]{1,0:T(8,128)(2,1)S(1)} %get-tuple-element.7.modes_ref, f32[128,8192]{1,0:T(8,128)S(1)} %get-tuple-element.8.free_ref, f32[2,64,300]{2,1,0:T(8,128)S(1)} %get-tuple-element.9.structure_ref), custom_call_target="tpu_custom_call" | custom-call | tf_op jit(solution)/shard_map/pallas_call | solution.py:422

commit v7 on v6

--- a/solution.py
+++ b/solution.py
@@ -21,7 +21,7 @@
     places = [()]
     for name in names:
         places = [place + (step,) for place in places for step in range(SIZES[name])]
-    return sorted(places[1:], key=lambda place: -hops(names, place))
+    return sorted(places[1:], key=lambda place: (-hops(names, place), place[-1]))
 
 
 def hops(names, place):

time: 36.3 us -> 36.3 us (level)
  no operation moved by 1% of the time
where the time goes in v7:
time: 36.3 us; the launch traced here: 36.2 us
  Pallas kernels  34.9 us (96%)
  between operations  1.29 us (4%)
    pallas_call x1, Pallas kernels, amplitudes(): pl.pallas_call(main_kernel, in_specs=[outside] * 2 + [pl.BlockSpec(memory...  32.8 us
    pallas_call x1, Pallas kernels, field(): pl.pallas_call(field_kernel, in_specs=[inside] * 4, out_specs=[pl.BlockSp...  2.16 us

profile of v7, /device:TPU:1, one launch (start us, length us, event | category | flops | bytes accessed | tf_op | source)
XLA Modules:
  0.0 36.2 jit_solution(77447348572965174)
XLA Ops:
  1.3 32.8 %shard_map.140 = (bf16[128,400]{1,0:T(8,128)(2,1)S(1)}, f32[2,64,300]{2,1,0:T(8,128)S(1)}, bf16[400,8192]{1,0:T(8,128)(2,1)S(1)}, f32[128,8192]{1,0:T(8,128)S(1)}) custom-call(bf16[400,8192]{1,0:T(8,128)(2,1)} %bitcast.2, bf16[300,1024]{1,0:T(8,128)(2,1)} %bitcast.3, s32[1]{0:T(128)S(6)} %copy.15.count_ref, s32[2048]{0:T(1024)} %fluid_hbm.1, s32[2048]{0:T(1024)} %node_hbm.1, ...), custom_call_target="tpu_custom_call" | custom-call | tf_op jit(solution)/shard_map/pallas_call | solution.py:346
  34.0 2.2 %shard_map.141 = (bf16[8192,128]{1,0:T(8,128)(2,1)}, f32[2,16,300]{2,1,0:T(8,128)}) custom-call(bf16[128,400]{1,0:T(8,128)(2,1)S(1)} %get-tuple-element.6.amps_ref, bf16[400,8192]{1,0:T(8,128)(2,1)S(1)} %get-tuple-element.7.modes_ref, f32[128,8192]{1,0:T(8,128)S(1)} %get-tuple-element.8.free_ref, f32[2,64,300]{2,1,0:T(8,128)S(1)} %get-tuple-element.9.structure_ref), custom_call_target="tpu_custom_call" | custom-call | tf_op jit(solution)/shard_map/pallas_call | solution.py:422

commit v8 on v7

--- a/solution.py
+++ b/solution.py
@@ -13,7 +13,7 @@
 STACK = ("z",)
 CHUNKS = 4
 PARTS = 8
-STEPS = 4
+STEPS = 8
 TAIL = 4
 
 
@@ -146,9 +146,10 @@
     amps_ref, structure_ref, modes_ref, free_ref = rest[7:11]
     shell_ref, fluid_ref, node_ref, area_ref = rest[11:15]
     terms = rest[15:22]
-    table_ref, rows_ref, pick_ref, area_rows_ref = rest[22:26]
-    part_ref, plane_ref, mine_ref, stack_ref, full_ref = rest[26:31]
-    modes_sem, small_sem, send_sem, recv_sem = rest[31:]
+    table_ref, total_ref = rest[22:24]
+    part_ref, plane_ref, mine_ref, stack_ref, full_ref = rest[24:29]
+    modes_sem, small_sem, send_sem, recv_sem = rest[29:33]
+    rows, picks = rest[33 : 33 + STEPS], rest[33 + STEPS :]
 
     cavity, depth = modes_ref.shape
     shells, shell_depth = shell_ref.shape
@@ -204,34 +205,32 @@
         copy.wait()
     count = count_ref[0]
 
-    def gather(step, carry):
-        here = pl.ds(pl.multiple_of(step * span, span), span)
+    for step in range(STEPS):
         slot = lax.broadcasted_iota(jnp.int32, (1, span), 1) + step * span
+        here = pl.ds(step * span, span)
         node = jnp.where(slot < count, node_ref[here].reshape(1, span), -1)
         number = lax.broadcasted_iota(jnp.int32, (shell_depth, span), 0)
         hot = jnp.where(number == node, 1.0, 0.0).astype(jnp.bfloat16)
-        pick_ref[:, here] = jnp.dot(
+        picks[step][...] = jnp.dot(
             shell_ref[...], hot, preferred_element_type=jnp.float32
         ).astype(jnp.bfloat16)
-        area = area_ref[here].reshape(1, span)
-        area_rows_ref[here, :] = jnp.broadcast_to(area, (LANES, span)).T
         for at in range(span):
-            row = step * span + at
-            rows_ref[pl.ds(pl.multiple_of(row * lane_blocks, lane_blocks), lane_blocks), :] = (
-                table_ref[pl.ds(fluid_ref[row] * lane_blocks, lane_blocks), :]
-            )
-        return carry
-
-    lax.fori_loop(0, STEPS, gather, 0)
-    area = area_rows_ref[...]
-    wet = jnp.concatenate(
-        [
-            (rows_ref[pl.ds(block, slots, stride=lane_blocks), :] * area).astype(jnp.bfloat16)
-            for block in range(lane_blocks)
-        ],
-        1,
-    )
-    total = jnp.dot(pick_ref[...], wet, preferred_element_type=jnp.float32)
+            rows[step][pl.ds(at * lane_blocks, lane_blocks), :] = table_ref[
+                pl.ds(fluid_ref[step * span + at] * lane_blocks, lane_blocks), :
+            ]
+        area = jnp.broadcast_to(area_ref[here].reshape(1, span), (LANES, span)).T
+        wet = jnp.concatenate(
+            [
+                (rows[step][pl.ds(block, span, stride=lane_blocks), :] * area).astype(
+                    jnp.bfloat16
+                )
+                for block in range(lane_blocks)
+            ],
+            1,
+        )
+        product = jnp.dot(picks[step][...], wet, preferred_element_type=jnp.float32)
+        total_ref[...] = product if step == 0 else total_ref[...] + product
+    total = total_ref[...]
     pack(total[:, :cavity], part_ref)
 
     size = mine_ref.shape[0]
@@ -364,9 +363,7 @@
         + [pltpu.VMEM(term.shape, term.dtype) for term in terms]
         + [
             pltpu.VMEM((depth * lane_blocks, LANES), jnp.float32),
-            pltpu.VMEM((slots * lane_blocks, LANES), jnp.float32),
-            pltpu.VMEM((shells, slots), jnp.bfloat16),
-            pltpu.VMEM((slots, LANES), jnp.float32),
+            pltpu.VMEM((shells, lane_blocks * LANES), jnp.float32),
             pltpu.VMEM((rows, LANES), jnp.bfloat16),
             pltpu.VMEM((planes, size, LANES), jnp.bfloat16),
             pltpu.VMEM((size, LANES), jnp.bfloat16),
@@ -376,7 +373,9 @@
             pltpu.SemaphoreType.DMA((4 + len(terms),)),
             pltpu.SemaphoreType.DMA((3,)),
             pltpu.SemaphoreType.DMA((3,)),
-        ],
+        ]
+        + [pltpu.VMEM((slots // STEPS * lane_blocks, LANES), jnp.float32)] * STEPS
+        + [pltpu.VMEM((shells, slots // STEPS), jnp.bfloat16)] * STEPS,
         compiler_params=pltpu.CompilerParams(
             collective_id=0, has_side_effects=True, vmem_limit_bytes=34 << 20
         ),

time: 36.3 us -> 35.8 us (0.986)
  Pallas kernels: 34.9 us -> 34.5 us
    pallas_call x1, Pallas kernels: 32.8 us -> 32.3 us  [amplitudes(): pl.pallas_call(main_kernel, in_specs=[outside] * 2 + [pl.BlockSpec(memory...]
where the time goes in v8:
time: 35.8 us; the launch traced here: 35.7 us
  Pallas kernels  34.5 us (96%)
  between operations  1.29 us (4%)
    pallas_call x1, Pallas kernels, amplitudes(): pl.pallas_call(main_kernel, in_specs=[outside] * 2 + [pl.BlockSpec(memory...  32.3 us
    pallas_call x1, Pallas kernels, field(): pl.pallas_call(field_kernel, in_specs=[inside] * 4, out_specs=[pl.BlockSp...  2.16 us

profile of v8, /device:TPU:1, one launch (start us, length us, event | category | flops | bytes accessed | tf_op | source)
XLA Modules:
  0.0 35.7 jit_solution(13766869653414682593)
XLA Ops:
  1.3 32.3 %shard_map.140 = (bf16[128,400]{1,0:T(8,128)(2,1)S(1)}, f32[2,64,300]{2,1,0:T(8,128)S(1)}, bf16[400,8192]{1,0:T(8,128)(2,1)S(1)}, f32[128,8192]{1,0:T(8,128)S(1)}) custom-call(bf16[400,8192]{1,0:T(8,128)(2,1)} %bitcast.2, bf16[300,1024]{1,0:T(8,128)(2,1)} %bitcast.3, s32[1]{0:T(128)S(6)} %copy.15.count_ref, s32[2048]{0:T(1024)} %fluid_hbm.1, s32[2048]{0:T(1024)} %node_hbm.1, ...), custom_call_target="tpu_custom_call" | custom-call | tf_op jit(solution)/shard_map/pallas_call | solution.py:345
  33.6 2.2 %shard_map.141 = (bf16[8192,128]{1,0:T(8,128)(2,1)}, f32[2,16,300]{2,1,0:T(8,128)}) custom-call(bf16[128,400]{1,0:T(8,128)(2,1)S(1)} %get-tuple-element.6.amps_ref, bf16[400,8192]{1,0:T(8,128)(2,1)S(1)} %get-tuple-element.7.modes_ref, f32[128,8192]{1,0:T(8,128)S(1)} %get-tuple-element.8.free_ref, f32[2,64,300]{2,1,0:T(8,128)S(1)} %get-tuple-element.9.structure_ref), custom_call_target="tpu_custom_call" | custom-call | tf_op jit(solution)/shard_map/pallas_call | solution.py:421
